TPU v7x, 512 devices: a whole 4x8x8 slice. The times are simulated.
512 devices in a mesh: lat: 16 (over y, core), lon: 32 (over z, x).
Axes of the slice: x: 4, y: 8, z: 8, core: 2. Of those that a mesh axis runs over, the one named last changes fastest.
Arguments:
- adjoint_in: float32 [4, 72, 128, 4096], P(None, None, 'lat', 'lon'), may hold values from -6 to 6
- wind_u: float32 [72, 128, 4096], P(None, 'lat', 'lon'), may hold values from -0.45 to 0.45
- wind_v: float32 [72, 128, 4096], P(None, 'lat', 'lon'), may hold values from -0.45 to 0.45
- diffusion: float32 [72, 128, 4096], P(None, 'lat', 'lon'), may hold values from 0.02 to 8
- kernel_rows: bfloat16 [72, 1048576], P(None, ('lat', 'lon')), may hold values from 0 to 1
- retrieval_misfit: bfloat16 [4, 1048576], P(None, ('lat', 'lon')), may hold values from -6 to 6
- retrieval_columns: int32 [1048576], P(('lat', 'lon')), may hold values from 0 to 32767, as said below
- retrieval_counts: int32 [512], P(('lat', 'lon')), may hold values from 128 to 2048, as said below
- station_cells: int32 [8192], P(('lat', 'lon')), may hold values from 0 to 1023
- station_misfit: float32 [4, 8192], P(None, ('lat', 'lon')), may hold values from -6 to 6
Outputs:
- adjoint_out: float32 [4, 72, 128, 4096], P(None, None, 'lat', 'lon')
Inputs may be any that keep to these rules, and one draw needn't show every extreme that they name: Only the first retrieval_counts slots of a device hold live retrievals; in each latitude band one device holds 2048. `retrieval_columns`: each value names a tile of the holding device's latitude band (value // 1024) and a cell of it (row times 128 plus column). Among the live retrievals of one device at most 128 name one tile, and in each band one tile is named by exactly 128 live retrievals of every device of the band.
All inputs are finite; a program needn't handle non-finite values.
Results may differ from a plain program's by a relative error of at most 0.0003.
Values may be sent and summed in bfloat16 or wider, within the bound.
No kernel may reach another device: no remote copies, remote signals or barrier semaphores. Data moves between devices by JAX's collectives and lax.ppermute only.
A program may use at most 128 MiB of HBM per device.

v0:
```python
import functools

import jax
import jax.numpy as jnp
from jax import lax
from jax.experimental import pallas as pl
from jax.experimental.pallas import tpu as pltpu
from jax.sharding import PartitionSpec as P

F32 = jnp.float32
BF16 = jnp.bfloat16
PARAMS = pltpu.CompilerParams(vmem_limit_bytes=56 << 20)
GROUP = 8


def lanes_iota():
    return lax.broadcasted_iota(jnp.int32, (8, 128), 1)


def rows_iota():
    return lax.broadcasted_iota(jnp.int32, (8, 128), 0)


def pack_kernel(count_ref, rows_ref, misfit_ref, columns_ref, out_ref):
    chunks = columns_ref.shape[0]
    tiles = out_ref.shape[0]
    count = count_ref[0]
    lane = lax.broadcasted_iota(jnp.int32, (1, 128), 1)
    tile = lax.broadcasted_iota(jnp.int32, (tiles, 128), 0)
    hits = []
    targets = []
    misc = []
    for j in range(chunks):
        column = columns_ref[j : j + 1, :]
        live = (lane + j * 128) < count
        target = jnp.where(live, column >> 10, -1)
        targets.append(target)
        hits.append((tile == target).astype(F32))
        cell = column & 1023
        misc.append(
            jnp.concatenate(
                [
                    misfit_ref[:, j * 128 : (j + 1) * 128].astype(F32),
                    (cell >> 7).astype(F32),
                    (cell & 127).astype(F32),
                    jnp.zeros((2, 128), F32),
                ],
                axis=0,
            )
        )
    before = lax.broadcasted_iota(jnp.int32, (128, 128), 0) < lax.broadcasted_iota(
        jnp.int32, (128, 128), 1
    )
    prefix = jnp.dot(
        jnp.concatenate(hits, axis=0).astype(BF16),
        before.astype(F32).astype(BF16),
        preferred_element_type=F32,
    )
    offset = jnp.zeros((tiles, 1), F32)
    ranks = []
    for j in range(chunks):
        rank = jnp.sum(
            hits[j] * (prefix[j * tiles : (j + 1) * tiles] + offset), axis=0, keepdims=True
        )
        ranks.append(rank)
        offset = offset + jnp.sum(hits[j], axis=1, keepdims=True)
    tail = jnp.concatenate(
        [rows_ref[64:72, :].astype(F32), jnp.concatenate(misc, axis=1)], axis=0
    ).astype(BF16)
    payload = jnp.concatenate([rows_ref[0:64, :], tail], axis=0)
    target = jnp.concatenate(targets, axis=1)
    rank = jnp.concatenate(ranks, axis=1)
    slot = lax.broadcasted_iota(jnp.int32, (128, chunks * 128), 0).astype(F32).astype(BF16)
    one = jnp.ones((128, chunks * 128), BF16)
    zero = jnp.zeros((128, chunks * 128), BF16)
    for pair in range(tiles // 2):
        parts = []
        for side in range(2):
            key = jnp.where(target == 2 * pair + side, rank, -1.0).astype(BF16)
            parts.append(jnp.where(slot == key, one, zero))
        chosen = jnp.concatenate(parts, axis=0)
        packed = lax.dot_general(
            payload, chosen, (((1,), (1,)), ((), ())), preferred_element_type=F32
        ).astype(BF16)
        out_ref[2 * pair] = packed[:, :128]
        out_ref[2 * pair + 1] = packed[:, 128:]


def rows_out(field_ref, up_ref, down_ref):
    count = up_ref.shape[0]
    up_ref[...] = field_ref[pl.ds(7, count, stride=8), :]
    down_ref[...] = field_ref[pl.ds(0, count, stride=8), :]


def columns_out(field_ref, east_ref, west_ref, levels):
    tracers = east_ref.shape[0]
    lane = lanes_iota()

    def group(g, carry):
        east, west = list(carry[0]), list(carry[1])
        for j in range(GROUP):
            level = g * GROUP + j
            here = lane == level
            for t in range(tracers):
                x = field_ref[pl.ds((t * levels + level) * 8, 8), :]
                east[t] = jnp.where(here, pltpu.roll(x, level + 1, 1), east[t])
                west[t] = jnp.where(here, pltpu.roll(x, level, 1), west[t])
        return tuple(east), tuple(west)

    zero = tuple(jnp.zeros((8, 128), F32) for _ in range(tracers))
    east, west = lax.fori_loop(0, levels // GROUP, group, (zero, zero))
    for t in range(tracers):
        east_ref[t] = east[t]
        west_ref[t] = west[t]


def prep_kernel(
    cells_ref,
    weights_ref,
    field_ref,
    diffusion_ref,
    started_ref,
    inverse_ref,
    up_ref,
    down_ref,
    east_ref,
    west_ref,
):
    levels = diffusion_ref.shape[0] // 8
    tracers = field_ref.shape[0] // (8 * levels)
    cell = rows_iota() * 128 + lanes_iota()
    started_ref[...] = field_ref[...]
    for t in range(tracers):
        total = jnp.zeros((8, 128), F32)
        for s in range(cells_ref.shape[0]):
            total = total + jnp.where(cell == cells_ref[s], weights_ref[t, s], 0.0)
        top = pl.ds(t * levels * 8, 8)
        started_ref[top, :] = field_ref[top, :] + total
    rows_out(started_ref, up_ref, down_ref)
    columns_out(started_ref, east_ref, west_ref, levels)

    def group(g, carry):
        below, inverse = carry
        for j in range(GROUP):
            spot = pl.ds((g * GROUP + j) * 8, 8)
            here = diffusion_ref[spot, :]
            inverse = 1.0 / (1.0 + below + here - below * below * inverse)
            inverse_ref[spot, :] = inverse
            below = here
        return below, inverse

    zero = jnp.zeros((8, 128), F32)
    lax.fori_loop(0, levels // GROUP, group, (zero, zero))


def step_body(field_ref, u_ref, v_ref, k_ref, inverse_ref, low, high, west, east, out_ref):
    levels = k_ref.shape[0] // 8
    tracers = field_ref.shape[0] // (8 * levels)
    lane = lanes_iota()
    row = rows_iota()
    last_lane, first_lane = lane == 127, lane == 0
    last_row, first_row = row == 7, row == 0
    zero = jnp.zeros((8, 128), F32)

    def forward(g, carry):
        below, state = carry[0], list(carry[1])
        for j in range(GROUP):
            level = g * GROUP + j
            spot = pl.ds(level * 8, 8)
            u, v = u_ref[spot, :], v_ref[spot, :]
            inverse = inverse_ref[spot, :]
            lift = below * inverse
            to_east = jnp.maximum(u, 0.0) * inverse
            to_west = jnp.maximum(-u, 0.0) * inverse
            to_north = jnp.maximum(v, 0.0) * inverse
            to_south = jnp.maximum(-v, 0.0) * inverse
            centre = inverse - jnp.abs(u) * inverse - jnp.abs(v) * inverse
            for t in range(tracers):
                at = t * levels + level
                x = field_ref[pl.ds(at * 8, 8), :]
                xe = jnp.where(
                    last_lane, pltpu.roll(east[t], 127 - level, 1), pltpu.roll(x, 127, 1)
                )
                xw = jnp.where(
                    first_lane, pltpu.roll(west[t], 128 - level, 1), pltpu.roll(x, 1, 1)
                )
                xn = jnp.where(last_row, high[pl.ds(at, 1), :], pltpu.roll(x, 7, 0))
                xs = jnp.where(first_row, low[pl.ds(at, 1), :], pltpu.roll(x, 1, 0))
                q = centre * x + to_east * xe + to_west * xw + to_north * xn + to_south * xs
                state[t] = q + lift * state[t]
                out_ref[pl.ds(at * 8, 8), :] = state[t]
            below = k_ref[spot, :]
        return below, tuple(state)

    lax.fori_loop(0, levels // GROUP, forward, (zero, (zero,) * tracers))

    def backward(g, state):
        state = list(state)
        for j in range(GROUP):
            level = levels - 1 - g * GROUP - j
            spot = pl.ds(level * 8, 8)
            upper = k_ref[spot, :] * inverse_ref[spot, :]
            for t in range(tracers):
                here = pl.ds((t * levels + level) * 8, 8)
                state[t] = out_ref[here, :] + upper * state[t]
                out_ref[here, :] = state[t]
        return tuple(state)

    lax.fori_loop(0, levels // GROUP, backward, (zero,) * tracers)


def step_kernel(
    field_ref,
    u_ref,
    v_ref,
    k_ref,
    inverse_ref,
    low_ref,
    high_ref,
    west_ref,
    east_ref,
    out_ref,
    *edge_refs,
):
    step_body(
        field_ref, u_ref, v_ref, k_ref, inverse_ref, low_ref, high_ref, west_ref, east_ref, out_ref
    )
    if edge_refs:
        up_ref, down_ref, east_out, west_out = edge_refs
        rows_out(out_ref, up_ref, down_ref)
        columns_out(out_ref, east_out, west_out, k_ref.shape[0] // 8)


def inject_kernel(received_ref, first_ref, out_ref, up_ref, down_ref, east_ref, west_ref):
    sources = received_ref.shape[0]
    tracers = east_ref.shape[0]
    levels = first_ref.shape[0] // (8 * tracers)
    rows = jnp.concatenate([received_ref[s, 0:levels, :] for s in range(sources)], axis=1)
    tail = jnp.concatenate([received_ref[s, 64:80, :] for s in range(sources)], axis=1).astype(F32)
    misfit = [tail[8 + t : 9 + t, :].astype(BF16) for t in range(tracers)]
    cell_row = tail[12:13, :]
    cell_lane = tail[13:14, :].astype(BF16)
    width = sources * 128
    lane = lax.broadcasted_iota(jnp.int32, (128, width), 0).astype(F32).astype(BF16)
    hot = jnp.where(lane == cell_lane, jnp.ones((), BF16), jnp.zeros((), BF16))
    for r in range(8):
        here = jnp.where(cell_row == r, 1.0, 0.0).astype(BF16)
        weighted = jnp.concatenate([hot * (here * misfit[t]) for t in range(tracers)], axis=0)
        forcing = lax.dot_general(
            rows, weighted, (((1,), (1,)), ((), ())), preferred_element_type=F32
        )
        for t in range(tracers):
            spot = pl.ds(t * levels * 8 + r, levels, stride=8)
            out_ref[spot, :] = first_ref[spot, :] + forcing[:, t * 128 : (t + 1) * 128]
    rows_out(out_ref, up_ref, down_ref)
    columns_out(out_ref, east_ref, west_ref, levels)


def exchange(edges):
    up, down, east, west = edges
    lat, lon = lax.axis_size("lat"), lax.axis_size("lon")
    north = [(i, i + 1) for i in range(lat - 1)]
    right = [(i, (i + 1) % lon) for i in range(lon)]
    low = lax.ppermute(up, "lat", north)
    high = lax.ppermute(down, "lat", [(b, a) for a, b in north])
    from_west = lax.ppermute(east, "lon", right)
    from_east = lax.ppermute(west, "lon", [(b, a) for a, b in right])
    return low, high, from_west, from_east


def body(
    adjoint_in,
    wind_u,
    wind_v,
    diffusion,
    kernel_rows,
    retrieval_misfit,
    retrieval_columns,
    retrieval_counts,
    station_cells,
    station_misfit,
):
    tracers, levels, lat_rows, lon_cells = adjoint_in.shape
    slots = kernel_rows.shape[1]
    tiles = lax.axis_size("lon")
    smem = pl.BlockSpec(memory_space=pltpu.SMEM)
    vmem = pl.BlockSpec(memory_space=pltpu.VMEM)
    call = functools.partial(pl.pallas_call, compiler_params=PARAMS)
    full = jax.ShapeDtypeStruct((tracers * levels * 8, 128), F32)
    planes = jax.ShapeDtypeStruct((levels * 8, 128), F32)
    edge_row = jax.ShapeDtypeStruct((tracers * levels, 128), F32)
    edge_column = jax.ShapeDtypeStruct((tracers, 8, 128), F32)
    edges = (edge_row, edge_row, edge_column, edge_column)

    packed = call(
        pack_kernel,
        out_shape=jax.ShapeDtypeStruct((tiles, 80, 128), BF16),
        in_specs=[smem, vmem, vmem, vmem],
        name="pack",
    )(retrieval_counts, kernel_rows, retrieval_misfit, retrieval_columns.reshape(slots // 128, 128))
    received = lax.all_to_all(packed, "lon", split_axis=0, concat_axis=0, tiled=True)

    field = adjoint_in.reshape(full.shape)
    u = wind_u.reshape(planes.shape)
    v = wind_v.reshape(planes.shape)
    k = diffusion.reshape(planes.shape)
    started, inverse, *sent = call(
        prep_kernel,
        out_shape=(full, planes) + edges,
        in_specs=[smem, smem, vmem, vmem],
        name="prep",
    )(station_cells, station_misfit, field, k)
    first = call(step_kernel, out_shape=full, name="first")(
        started, u, v, k, inverse, *exchange(sent)
    )
    injected, *sent = call(inject_kernel, out_shape=(full,) + edges, name="inject")(received, first)
    second, *sent = call(step_kernel, out_shape=(full,) + edges, name="second")(
        injected, u, v, k, inverse, *exchange(sent)
    )
    last = call(step_kernel, out_shape=full, name="last")(
        second, u, v, k, inverse, *exchange(sent)
    )
    return last.reshape(adjoint_in.shape)


def solution(mesh):
    return jax.shard_map(
        body,
        mesh=mesh,
        in_specs=(
            P(None, None, "lat", "lon"),
            P(None, "lat", "lon"),
            P(None, "lat", "lon"),
            P(None, "lat", "lon"),
            P(None, ("lat", "lon")),
            P(None, ("lat", "lon")),
            P(("lat", "lon")),
            P(("lat", "lon")),
            P(("lat", "lon")),
            P(None, ("lat", "lon")),
        ),
        out_specs=P(None, None, "lat", "lon"),
        check_vma=False,
    )
```

profile of v0, /device:TPU:230, one launch (start us, length us, event | category | flops | bytes accessed | tf_op | source)
XLA Modules:
  0.0 113.5 jit_solution(5309019710526120443)
XLA Ops:
  0.7 7.1 %pack.1 = bf16[32,80,128]{2,1,0:T(8,128)(2,1)} custom-call(s32[1]{0:T(128)S(6)} %copy.11.count_ref, bf16[72,2048]{1,0:T(8,128)(2,1)} %rows_ref.1, bf16[4,2048]{1,0:T(4,128)(2,1)} %misfit_ref.1, s32[16,128]{1,0:T(8,128)} %bitcast.17), custom_call_target="tpu_custom_call" | custom-call | tf_op jit(solution)/shard_map/pack/pallas_call | solution.py:295
  7.8 10.7 %all-to-all-start = ((bf16[32,80,128]{2,1,0:T(8,128)(2,1)}), bf16[32,80,128]{2,1,0:T(8,128)(2,1)S(1)}, u32[]{:S(2)}, u32[]{:S(2)}) async-start(bf16[32,80,128]{2,1,0:T(8,128)(2,1)} %pack.1), calls=%async_computation | async-start | bytes 1310720 | tf_op jit(solution)/shard_map/all_to_all | solution.py:301
  18.5 4.4 %prep.1 = (f32[2304,128]{1,0:T(8,128)}, f32[576,128]{1,0:T(8,128)}, f32[288,128]{1,0:T(8,128)}, f32[288,128]{1,0:T(8,128)}, f32[4,8,128]{2,1,0:T(8,128)}, /*index=5*/f32[4,8,128]{2,1,0:T(8,128)}) custom-call(s32[16]{0:T(128)} %cells_ref.1, f32[4,16]{1,0:T(4,128)} %weights_ref.1, f32[2304,128]{1,0:T(8,128)} %bitcast.16, f32[576,128]{1,0:T(8,128)} %bitcast.6), custom_call_target="tpu_custom_call" | custom-call | tf_op jit(solution)/shard_map/prep/pallas_call | solution.py:307
  22.9 1.9 %collective-permute-start = (f32[288,128]{1,0:T(8,128)}, f32[288,128]{1,0:T(8,128)S(1)}, u32[]{:S(2)}, u32[]{:S(2)}) collective-permute-start(f32[288,128]{1,0:T(8,128)} %get-tuple-element.23), channel_id=1, source_target_pairs={{0,32},{32,64},{64,96},{96,128},{128,160},{160,192},{192,224},{224... | collective-permute-start | bytes 442376 | tf_op jit(solution)/shard_map/ppermute | solution.py:264
  24.8 4.9 %collective-permute-start.1 = (f32[288,128]{1,0:T(8,128)}, f32[288,128]{1,0:T(8,128)S(1)}, u32[]{:S(2)}, u32[]{:S(2)}) collective-permute-start(f32[288,128]{1,0:T(8,128)} %get-tuple-element.24), channel_id=1, source_target_pairs={{32,0},{64,32},{96,64},{128,96},{160,128},{192,160},{224,192},{256... | collective-permute-start | bytes 442376 | tf_op jit(solution)/shard_map/ppermute | solution.py:265
  29.7 4.6 %collective-permute-start.2 = (f32[4,8,128]{2,1,0:T(8,128)}, f32[4,8,128]{2,1,0:T(8,128)S(1)}, u32[]{:S(2)}, u32[]{:S(2)}) collective-permute-start(f32[4,8,128]{2,1,0:T(8,128)} %get-tuple-element.25), channel_id=1, source_target_pairs={{0,1},{1,2},{2,3},{3,4},{4,5},{5,6},{6,7},{7,8},{8,9},{9,10},{10,1... | collective-permute-start | bytes 49160 | tf_op jit(solution)/shard_map/ppermute | solution.py:266
  34.3 1.9 %collective-permute-start.3 = (f32[4,8,128]{2,1,0:T(8,128)}, f32[4,8,128]{2,1,0:T(8,128)S(1)}, u32[]{:S(2)}, u32[]{:S(2)}) collective-permute-start(f32[4,8,128]{2,1,0:T(8,128)} %get-tuple-element.26), channel_id=1, source_target_pairs={{1,0},{2,1},{3,2},{4,3},{5,4},{6,5},{7,6},{8,7},{9,8},{10,9},{11,1... | collective-permute-start | bytes 49160 | tf_op jit(solution)/shard_map/ppermute | solution.py:267
  36.2 0.0 collective-permute-done.2.west_ref
  36.2 0.0 copy-start.10
  36.2 7.2 %collective-permute-done.3.east_ref = f32[4,8,128]{2,1,0:T(8,128)S(1)} collective-permute-done((f32[4,8,128]{2,1,0:T(8,128)}, f32[4,8,128]{2,1,0:T(8,128)S(1)}, u32[]{:S(2)}, u32[]{:S(2)}) %collective-permute-start.3) | collective-permute-done | bytes 16416 | tf_op jit(solution)/shard_map/ppermute | solution.py:267
  43.4 0.0 collective-permute-done.low_ref
  43.4 0.0 collective-permute-done.1.high_ref
  43.4 0.0 copy-start.6
  43.5 0.0 copy-done.10
  43.5 0.6 copy-done.12
  44.0 0.1 copy-done.4
  44.1 0.1 copy-done.6
  44.2 5.3 %first.1.first_ref = f32[2304,128]{1,0:T(8,128)} custom-call(f32[2304,128]{1,0:T(8,128)} %get-tuple-element.21.field_ref, f32[576,128]{1,0:T(8,128)} %bitcast.10, f32[576,128]{1,0:T(8,128)} %bitcast.13, f32[576,128]{1,0:T(8,128)} %bitcast.7, f32[576,128]{1,0:T(8,128)} %get-tuple-element.22.inverse_ref, f32[288,128]{1,0:T(8,128)} %copy-done.4, ...), custom_call_target="tpu_custom_call" | custom-call | tf_op jit(solution)/shard_map/first/pallas_call | solution.py:313
  49.5 0.0 all-to-all-done.received_ref
  49.5 0.8 copy-done
  50.3 14.1 %inject.1 = (f32[2304,128]{1,0:T(8,128)}, f32[288,128]{1,0:T(8,128)}, f32[288,128]{1,0:T(8,128)}, f32[4,8,128]{2,1,0:T(8,128)}, f32[4,8,128]{2,1,0:T(8,128)}) custom-call(bf16[32,80,128]{2,1,0:T(8,128)(2,1)} %copy-done, f32[2304,128]{1,0:T(8,128)} %first.1.first_ref), custom_call_target="tpu_custom_call" | custom-call | tf_op jit(solution)/shard_map/inject/pallas_call | solution.py:316
  64.4 1.9 %collective-permute-start.4 = (f32[288,128]{1,0:T(8,128)}, f32[288,128]{1,0:T(8,128)S(1)}, u32[]{:S(2)}, u32[]{:S(2)}) collective-permute-start(f32[288,128]{1,0:T(8,128)} %get-tuple-element.28), channel_id=1, source_target_pairs={{0,32},{32,64},{64,96},{96,128},{128,160},{160,192},{192,224},{224... | collective-permute-start | bytes 442376 | tf_op jit(solution)/shard_map/ppermute | solution.py:264
  66.4 4.9 %collective-permute-start.5 = (f32[288,128]{1,0:T(8,128)}, f32[288,128]{1,0:T(8,128)S(1)}, u32[]{:S(2)}, u32[]{:S(2)}) collective-permute-start(f32[288,128]{1,0:T(8,128)} %get-tuple-element.29), channel_id=1, source_target_pairs={{32,0},{64,32},{96,64},{128,96},{160,128},{192,160},{224,192},{256... | collective-permute-start | bytes 442376 | tf_op jit(solution)/shard_map/ppermute | solution.py:265
  71.2 1.9 %collective-permute-start.6 = (f32[4,8,128]{2,1,0:T(8,128)}, f32[4,8,128]{2,1,0:T(8,128)S(1)}, u32[]{:S(2)}, u32[]{:S(2)}) collective-permute-start(f32[4,8,128]{2,1,0:T(8,128)} %get-tuple-element.30), channel_id=1, source_target_pairs={{0,1},{1,2},{2,3},{3,4},{4,5},{5,6},{6,7},{7,8},{8,9},{9,10},{10,1... | collective-permute-start | bytes 49160 | tf_op jit(solution)/shard_map/ppermute | solution.py:266
  73.1 3.9 %collective-permute-start.7 = (f32[4,8,128]{2,1,0:T(8,128)}, f32[4,8,128]{2,1,0:T(8,128)S(1)}, u32[]{:S(2)}, u32[]{:S(2)}) collective-permute-start(f32[4,8,128]{2,1,0:T(8,128)} %get-tuple-element.31), channel_id=1, source_target_pairs={{1,0},{2,1},{3,2},{4,3},{5,4},{6,5},{7,6},{8,7},{9,8},{10,9},{11,1... | collective-permute-start | bytes 49160 | tf_op jit(solution)/shard_map/ppermute | solution.py:267
  77.1 0.0 collective-permute-done.6.west_ref
  77.1 5.2 %collective-permute-done.7.east_ref = f32[4,8,128]{2,1,0:T(8,128)S(1)} collective-permute-done((f32[4,8,128]{2,1,0:T(8,128)}, f32[4,8,128]{2,1,0:T(8,128)S(1)}, u32[]{:S(2)}, u32[]{:S(2)}) %collective-permute-start.7) | collective-permute-done | bytes 16416 | tf_op jit(solution)/shard_map/ppermute | solution.py:267
  82.3 0.0 collective-permute-done.4.low_ref
  82.3 0.0 collective-permute-done.5.high_ref
  82.3 0.6 copy-done.8
  82.9 0.1 copy-done.1
  83.0 0.1 copy-done.2
  83.0 6.6 %second.1 = (f32[2304,128]{1,0:T(8,128)}, f32[288,128]{1,0:T(8,128)}, f32[288,128]{1,0:T(8,128)}, f32[4,8,128]{2,1,0:T(8,128)}, f32[4,8,128]{2,1,0:T(8,128)}) custom-call(f32[2304,128]{1,0:T(8,128)} %get-tuple-element.27.field_ref, f32[576,128]{1,0:T(8,128)} %bitcast.11, f32[576,128]{1,0:T(8,128)} %bitcast.14, f32[576,128]{1,0:T(8,128)} %bitcast.8, ...), custom_call_target="tpu_custom_call" | custom-call | tf_op jit(solution)/shard_map/second/pallas_call | solution.py:317
  89.6 1.9 %collective-permute-start.8 = (f32[288,128]{1,0:T(8,128)}, f32[288,128]{1,0:T(8,128)S(1)}, u32[]{:S(2)}, u32[]{:S(2)}) collective-permute-start(f32[288,128]{1,0:T(8,128)} %get-tuple-element.33), channel_id=1, source_target_pairs={{0,32},{32,64},{64,96},{96,128},{128,160},{160,192},{192,224},{224... | collective-permute-start | bytes 442376 | tf_op jit(solution)/shard_map/ppermute | solution.py:264
  91.5 4.9 %collective-permute-start.9 = (f32[288,128]{1,0:T(8,128)}, f32[288,128]{1,0:T(8,128)S(1)}, u32[]{:S(2)}, u32[]{:S(2)}) collective-permute-start(f32[288,128]{1,0:T(8,128)} %get-tuple-element.34), channel_id=1, source_target_pairs={{32,0},{64,32},{96,64},{128,96},{160,128},{192,160},{224,192},{256... | collective-permute-start | bytes 442376 | tf_op jit(solution)/shard_map/ppermute | solution.py:265
  96.4 1.9 %collective-permute-start.10 = (f32[4,8,128]{2,1,0:T(8,128)}, f32[4,8,128]{2,1,0:T(8,128)S(1)}, u32[]{:S(2)}, u32[]{:S(2)}) collective-permute-start(f32[4,8,128]{2,1,0:T(8,128)} %get-tuple-element.35), channel_id=1, source_target_pairs={{0,1},{1,2},{2,3},{3,4},{4,5},{5,6},{6,7},{7,8},{8,9},{9,10},{10,1... | collective-permute-start | bytes 49160 | tf_op jit(solution)/shard_map/ppermute | solution.py:266
  98.3 3.9 %collective-permute-start.11 = (f32[4,8,128]{2,1,0:T(8,128)}, f32[4,8,128]{2,1,0:T(8,128)S(1)}, u32[]{:S(2)}, u32[]{:S(2)}) collective-permute-start(f32[4,8,128]{2,1,0:T(8,128)} %get-tuple-element.36), channel_id=1, source_target_pairs={{1,0},{2,1},{3,2},{4,3},{5,4},{6,5},{7,6},{8,7},{9,8},{10,9},{11,1... | collective-permute-start | bytes 49160 | tf_op jit(solution)/shard_map/ppermute | solution.py:267
  102.3 0.0 collective-permute-done.10.west_ref
  102.3 0.0 copy-start.9
  102.3 5.2 %collective-permute-done.11.east_ref = f32[4,8,128]{2,1,0:T(8,128)S(1)} collective-permute-done((f32[4,8,128]{2,1,0:T(8,128)}, f32[4,8,128]{2,1,0:T(8,128)S(1)}, u32[]{:S(2)}, u32[]{:S(2)}) %collective-permute-start.11) | collective-permute-done | bytes 16416 | tf_op jit(solution)/shard_map/ppermute | solution.py:267
  107.5 0.0 collective-permute-done.8.low_ref
  107.5 0.0 collective-permute-done.9.high_ref
  107.5 0.0 copy-start.5
  107.5 0.0 copy-done.9
  107.5 0.6 copy-done.11
  108.1 0.1 copy-done.3
  108.1 0.1 copy-done.5
  108.2 5.3 %last.1 = f32[2304,128]{1,0:T(8,128)} custom-call(f32[2304,128]{1,0:T(8,128)} %get-tuple-element.32.field_ref, f32[576,128]{1,0:T(8,128)} %bitcast.12, f32[576,128]{1,0:T(8,128)} %bitcast.15, f32[576,128]{1,0:T(8,128)} %bitcast.9, f32[576,128]{1,0:T(8,128)} %get-tuple-element.22.inverse_ref, f32[288,128]{1,0:T(8,128)} %copy-done.3, f32[288,128]{1,0:T(8,128)} %copy-done.5, ...), custom_call_target="tpu_custom_call" | custom-call | tf_op jit(solution)/shard_map/last/pallas_call | solution.py:320
  (10 shorter events, 0.0 us)
Async XLA Ops:
  7.8 41.7 %all-to-all-start = ((bf16[32,80,128]{2,1,0:T(8,128)(2,1)}), bf16[32,80,128]{2,1,0:T(8,128)(2,1)S(1)}, u32[]{:S(2)}, u32[]{:S(2)}) async-start(bf16[32,80,128]{2,1,0:T(8,128)(2,1)} %pack.1), calls=%async_computation | async-start | bytes 1310720 | tf_op jit(solution)/shard_map/all_to_all | solution.py:301
  22.9 20.5 %collective-permute-start = (f32[288,128]{1,0:T(8,128)}, f32[288,128]{1,0:T(8,128)S(1)}, u32[]{:S(2)}, u32[]{:S(2)}) collective-permute-start(f32[288,128]{1,0:T(8,128)} %get-tuple-element.23), channel_id=1, source_target_pairs={{0,32},{32,64},{64,96},{96,128},{128,160},{160,192},{192,224},{224... | collective-permute-start | bytes 442376 | tf_op jit(solution)/shard_map/ppermute | solution.py:264
  24.8 18.6 %collective-permute-start.1 = (f32[288,128]{1,0:T(8,128)}, f32[288,128]{1,0:T(8,128)S(1)}, u32[]{:S(2)}, u32[]{:S(2)}) collective-permute-start(f32[288,128]{1,0:T(8,128)} %get-tuple-element.24), channel_id=1, source_target_pairs={{32,0},{64,32},{96,64},{128,96},{160,128},{192,160},{224,192},{256... | collective-permute-start | bytes 442376 | tf_op jit(solution)/shard_map/ppermute | solution.py:265
  29.7 6.5 %collective-permute-start.2 = (f32[4,8,128]{2,1,0:T(8,128)}, f32[4,8,128]{2,1,0:T(8,128)S(1)}, u32[]{:S(2)}, u32[]{:S(2)}) collective-permute-start(f32[4,8,128]{2,1,0:T(8,128)} %get-tuple-element.25), channel_id=1, source_target_pairs={{0,1},{1,2},{2,3},{3,4},{4,5},{5,6},{6,7},{7,8},{8,9},{9,10},{10,1... | collective-permute-start | bytes 49160 | tf_op jit(solution)/shard_map/ppermute | solution.py:266
  34.3 9.2 %collective-permute-start.3 = (f32[4,8,128]{2,1,0:T(8,128)}, f32[4,8,128]{2,1,0:T(8,128)S(1)}, u32[]{:S(2)}, u32[]{:S(2)}) collective-permute-start(f32[4,8,128]{2,1,0:T(8,128)} %get-tuple-element.26), channel_id=1, source_target_pairs={{1,0},{2,1},{3,2},{4,3},{5,4},{6,5},{7,6},{8,7},{9,8},{10,9},{11,1... | collective-permute-start | bytes 49160 | tf_op jit(solution)/shard_map/ppermute | solution.py:267
  36.2 7.3 %copy-start.10 = (f32[4,8,128]{2,1,0:T(8,128)}, f32[4,8,128]{2,1,0:T(8,128)S(1)}, u32[]{:S(2)}) copy-start(f32[4,8,128]{2,1,0:T(8,128)S(1)} %collective-permute-done.2.west_ref) | copy-start | bytes 49156
  43.4 0.6 copy-start.12
  43.4 0.7 copy-start.4
  43.4 0.7 copy-start.6
  49.5 0.8 copy-start
  64.4 17.9 %collective-permute-start.4 = (f32[288,128]{1,0:T(8,128)}, f32[288,128]{1,0:T(8,128)S(1)}, u32[]{:S(2)}, u32[]{:S(2)}) collective-permute-start(f32[288,128]{1,0:T(8,128)} %get-tuple-element.28), channel_id=1, source_target_pairs={{0,32},{32,64},{64,96},{96,128},{128,160},{160,192},{192,224},{224... | collective-permute-start | bytes 442376 | tf_op jit(solution)/shard_map/ppermute | solution.py:264
  66.4 16.0 %collective-permute-start.5 = (f32[288,128]{1,0:T(8,128)}, f32[288,128]{1,0:T(8,128)S(1)}, u32[]{:S(2)}, u32[]{:S(2)}) collective-permute-start(f32[288,128]{1,0:T(8,128)} %get-tuple-element.29), channel_id=1, source_target_pairs={{32,0},{64,32},{96,64},{128,96},{160,128},{192,160},{224,192},{256... | collective-permute-start | bytes 442376 | tf_op jit(solution)/shard_map/ppermute | solution.py:265
  71.2 5.9 %collective-permute-start.6 = (f32[4,8,128]{2,1,0:T(8,128)}, f32[4,8,128]{2,1,0:T(8,128)S(1)}, u32[]{:S(2)}, u32[]{:S(2)}) collective-permute-start(f32[4,8,128]{2,1,0:T(8,128)} %get-tuple-element.30), channel_id=1, source_target_pairs={{0,1},{1,2},{2,3},{3,4},{4,5},{5,6},{6,7},{7,8},{8,9},{9,10},{10,1... | collective-permute-start | bytes 49160 | tf_op jit(solution)/shard_map/ppermute | solution.py:266
  73.1 9.2 %collective-permute-start.7 = (f32[4,8,128]{2,1,0:T(8,128)}, f32[4,8,128]{2,1,0:T(8,128)S(1)}, u32[]{:S(2)}, u32[]{:S(2)}) collective-permute-start(f32[4,8,128]{2,1,0:T(8,128)} %get-tuple-element.31), channel_id=1, source_target_pairs={{1,0},{2,1},{3,2},{4,3},{5,4},{6,5},{7,6},{8,7},{9,8},{10,9},{11,1... | collective-permute-start | bytes 49160 | tf_op jit(solution)/shard_map/ppermute | solution.py:267
  77.1 5.2 %copy-start.7 = (f32[4,8,128]{2,1,0:T(8,128)}, f32[4,8,128]{2,1,0:T(8,128)S(1)}, u32[]{:S(2)}) copy-start(f32[4,8,128]{2,1,0:T(8,128)S(1)} %collective-permute-done.6.west_ref) | copy-start | bytes 49156
  82.3 0.6 copy-start.8
  82.3 0.7 copy-start.1
  82.3 0.7 copy-start.2
  89.6 17.9 %collective-permute-start.8 = (f32[288,128]{1,0:T(8,128)}, f32[288,128]{1,0:T(8,128)S(1)}, u32[]{:S(2)}, u32[]{:S(2)}) collective-permute-start(f32[288,128]{1,0:T(8,128)} %get-tuple-element.33), channel_id=1, source_target_pairs={{0,32},{32,64},{64,96},{96,128},{128,160},{160,192},{192,224},{224... | collective-permute-start | bytes 442376 | tf_op jit(solution)/shard_map/ppermute | solution.py:264
  91.5 16.0 %collective-permute-start.9 = (f32[288,128]{1,0:T(8,128)}, f32[288,128]{1,0:T(8,128)S(1)}, u32[]{:S(2)}, u32[]{:S(2)}) collective-permute-start(f32[288,128]{1,0:T(8,128)} %get-tuple-element.34), channel_id=1, source_target_pairs={{32,0},{64,32},{96,64},{128,96},{160,128},{192,160},{224,192},{256... | collective-permute-start | bytes 442376 | tf_op jit(solution)/shard_map/ppermute | solution.py:265
  96.4 5.9 %collective-permute-start.10 = (f32[4,8,128]{2,1,0:T(8,128)}, f32[4,8,128]{2,1,0:T(8,128)S(1)}, u32[]{:S(2)}, u32[]{:S(2)}) collective-permute-start(f32[4,8,128]{2,1,0:T(8,128)} %get-tuple-element.35), channel_id=1, source_target_pairs={{0,1},{1,2},{2,3},{3,4},{4,5},{5,6},{6,7},{7,8},{8,9},{9,10},{10,1... | collective-permute-start | bytes 49160 | tf_op jit(solution)/shard_map/ppermute | solution.py:266
  98.3 9.2 %collective-permute-start.11 = (f32[4,8,128]{2,1,0:T(8,128)}, f32[4,8,128]{2,1,0:T(8,128)S(1)}, u32[]{:S(2)}, u32[]{:S(2)}) collective-permute-start(f32[4,8,128]{2,1,0:T(8,128)} %get-tuple-element.36), channel_id=1, source_target_pairs={{1,0},{2,1},{3,2},{4,3},{5,4},{6,5},{7,6},{8,7},{9,8},{10,9},{11,1... | collective-permute-start | bytes 49160 | tf_op jit(solution)/shard_map/ppermute | solution.py:267
  102.3 5.2 %copy-start.9 = (f32[4,8,128]{2,1,0:T(8,128)}, f32[4,8,128]{2,1,0:T(8,128)S(1)}, u32[]{:S(2)}) copy-start(f32[4,8,128]{2,1,0:T(8,128)S(1)} %collective-permute-done.10.west_ref) | copy-start | bytes 49156
  107.5 0.6 copy-start.11
  107.5 0.7 copy-start.3
  107.5 0.7 copy-start.5
where the time goes:
time: 114 us
  starting transfers between devices  49.1 us (43%)
  Pallas kernels  42.9 us (38%)
  waiting for transfers between devices  17.7 us (16%)
  local copies, waits for them, and re-layouts  2.94 us (3%)
    ppermute x3, waiting for transfers between devices, exchange(): from_east = lax.ppermute(west, 'lon', [(b, a) for a, b in right])  17.6 us
    ppermute x3, starting transfers between devices, exchange(): high = lax.ppermute(down, 'lat', [(b, a) for a, b in north])  14.6 us
    pallas_call x1, Pallas kernels, body(): call(inject_kernel, out_shape=(full,) + edges, name='inject')  14.1 us
    all_to_all x1, starting transfers between devices, body(): lax.all_to_all(packed, 'lon', split_axis=0, concat_axis=0, tiled=True)  10.7 us
    ppermute x3, starting transfers between devices, exchange(): from_east = lax.ppermute(west, 'lon', [(b, a) for a, b in right])  9.76 us
    ppermute x3, starting transfers between devices, exchange(): from_west = lax.ppermute(east, 'lon', right)  8.42 us
    pallas_call x1, Pallas kernels, body(): call(pack_kernel, out_shape=jax.ShapeDtypeStruct((tiles, 80, 128), BF16),...  7.15 us
    pallas_call x1, Pallas kernels, body(): call(step_kernel, out_shape=(full,) + edges, name='second')  6.6 us
  transfers between devices with their start and end apart: 13, of which 3 were waited for; matrix products, arithmetic and copies ran while one was open for 0% of the time, Pallas kernels for 9%

commit v1 on v0

v1 whole, which is shorter than its diff:
```python
import jax
import jax.numpy as jnp
from jax import lax
from jax.experimental import pallas as pl
from jax.experimental.pallas import tpu as pltpu
from jax.sharding import PartitionSpec as P

F32 = jnp.float32
BF16 = jnp.bfloat16
GROUP = 8


def vmem_call(kernel, *, out_shape, smem=0, scratch=(), limit=16, name):
    is_tuple = isinstance(out_shape, tuple)
    outs = out_shape if is_tuple else (out_shape,)
    outs = tuple(pltpu.VMEM(o.shape, o.dtype) for o in outs)

    def run(*args):
        args = args[:smem] + tuple(
            pltpu.with_memory_space_constraint(a, pltpu.VMEM) for a in args[smem:]
        )
        specs = [pl.BlockSpec(memory_space=pltpu.SMEM)] * smem
        specs += [pl.BlockSpec(memory_space=pltpu.VMEM)] * (len(args) - smem)
        return pl.pallas_call(
            kernel,
            out_shape=outs if is_tuple else outs[0],
            in_specs=specs,
            scratch_shapes=[pltpu.VMEM(o.shape, o.dtype) for o in scratch],
            compiler_params=pltpu.CompilerParams(vmem_limit_bytes=limit << 20),
            name=name,
        )(*args)

    return run


def lanes_iota():
    return lax.broadcasted_iota(jnp.int32, (8, 128), 1)


def rows_iota():
    return lax.broadcasted_iota(jnp.int32, (8, 128), 0)


def pack_kernel(count_ref, rows_ref, misfit_ref, columns_ref, out_ref):
    chunks = columns_ref.shape[0]
    tiles = out_ref.shape[0]
    count = count_ref[0]
    lane = lax.broadcasted_iota(jnp.int32, (1, 128), 1)
    tile = lax.broadcasted_iota(jnp.int32, (tiles, 128), 0)
    hits = []
    targets = []
    misc = []
    for j in range(chunks):
        column = columns_ref[j : j + 1, :]
        live = (lane + j * 128) < count
        target = jnp.where(live, column >> 10, -1)
        targets.append(target)
        hits.append((tile == target).astype(F32))
        cell = column & 1023
        misc.append(
            jnp.concatenate(
                [
                    misfit_ref[:, j * 128 : (j + 1) * 128].astype(F32),
                    (cell >> 7).astype(F32),
                    (cell & 127).astype(F32),
                    jnp.zeros((2, 128), F32),
                ],
                axis=0,
            )
        )
    before = lax.broadcasted_iota(jnp.int32, (128, 128), 0) < lax.broadcasted_iota(
        jnp.int32, (128, 128), 1
    )
    prefix = jnp.dot(
        jnp.concatenate(hits, axis=0).astype(BF16),
        before.astype(F32).astype(BF16),
        preferred_element_type=F32,
    )
    offset = jnp.zeros((tiles, 1), F32)
    ranks = []
    for j in range(chunks):
        rank = jnp.sum(
            hits[j] * (prefix[j * tiles : (j + 1) * tiles] + offset), axis=0, keepdims=True
        )
        ranks.append(rank)
        offset = offset + jnp.sum(hits[j], axis=1, keepdims=True)
    tail = jnp.concatenate(
        [rows_ref[64:72, :].astype(F32), jnp.concatenate(misc, axis=1)], axis=0
    ).astype(BF16)
    payload = jnp.concatenate([rows_ref[0:64, :], tail], axis=0)
    rank = jnp.concatenate(ranks, axis=0).T
    target = jnp.concatenate(targets, axis=0).astype(F32).T
    slot = lax.broadcasted_iota(jnp.int32, (128, 128), 1).astype(F32).astype(BF16)
    one, zero = jnp.ones((), BF16), jnp.zeros((), BF16)
    spread = [
        [jnp.broadcast_to(x[:, j : j + 1], (128, 128)).astype(BF16) for j in range(chunks)]
        for x in (rank, target)
    ]
    hot = jnp.concatenate([jnp.where(x == slot, one, zero) for x in spread[0]], axis=0)
    target = jnp.concatenate(spread[1], axis=0)
    for pair in range(tiles // 2):
        chosen = [
            jnp.where(target == jnp.asarray(2.0 * pair + side, BF16), hot, zero)
            for side in range(2)
        ]
        packed = jnp.dot(
            payload, jnp.concatenate(chosen, axis=1), preferred_element_type=F32
        ).astype(BF16)
        out_ref[2 * pair] = packed[:, :128]
        out_ref[2 * pair + 1] = packed[:, 128:]


def add_column(total, x, source, target, width):
    lane = lanes_iota()
    here = (lane >= target) & (lane < target + width)
    return jnp.where(here, pltpu.roll(x, (target - source + 128) % 128, 1), total)


def prep_kernel(
    cells_ref,
    weights_ref,
    field_ref,
    u_ref,
    v_ref,
    k_ref,
    surface_ref,
    up_ref,
    down_ref,
    east_ref,
    west_ref,
):
    levels = k_ref.shape[0] // 8
    tracers = field_ref.shape[0] // (8 * levels)
    cell = rows_iota() * 128 + lanes_iota()
    surface = []
    for t in range(tracers):
        total = jnp.zeros((8, 128), F32)
        for s in range(cells_ref.shape[0]):
            total = total + jnp.where(cell == cells_ref[s], weights_ref[t, s], 0.0)
        surface.append(total)
        surface_ref[t] = total
    count = tracers * levels
    for row, ref in ((7, up_ref), (0, down_ref)):
        ref[0:count, :] = field_ref[pl.ds(row, count, stride=8), :]
        for t in range(tracers):
            top = slice(t * levels, t * levels + 1)
            ref[top, :] = ref[top, :] + surface[t][row : row + 1, :]
        for i, plane in enumerate((u_ref, v_ref, k_ref)):
            at = count + i * levels
            ref[at : at + levels, :] = plane[pl.ds(row, levels, stride=8), :]

    def group(g, carry):
        east, west = list(carry[0]), list(carry[1])
        for j in range(GROUP):
            level = g * GROUP + j
            spot = pl.ds(level * 8, 8)
            values = [field_ref[pl.ds((t * levels + level) * 8, 8), :] for t in range(tracers)]
            if j == 0:
                values = [x + jnp.where(g == 0, add, 0.0) for x, add in zip(values, surface)]
            values += [u_ref[spot, :], v_ref[spot, :], k_ref[spot, :]]
            for i, x in enumerate(values):
                east[i] = add_column(east[i], x, 127, level, 1)
                west[i] = add_column(west[i], x, 0, level, 1)
        return tuple(east), tuple(west)

    zeros = (jnp.zeros((8, 128), F32),) * (tracers + 3)
    east, west = lax.fori_loop(0, levels // GROUP, group, (zeros, zeros))
    for i in range(tracers + 3):
        east_ref[i] = east[i]
        west_ref[i] = west[i]


def factor_kernel(k_ref, inverse_ref):
    def group(g, carry):
        below, inverse = carry
        for j in range(GROUP):
            spot = pl.ds((g * GROUP + j) * 8, 8)
            here = k_ref[spot, :]
            inverse = 1.0 / (1.0 + below + here - below * below * inverse)
            inverse_ref[spot, :] = inverse
            below = here
        return below, inverse

    zero = jnp.zeros((8, 128), F32)
    lax.fori_loop(0, k_ref.shape[0] // (8 * GROUP), group, (zero, zero))


class Advection:
    def __init__(self, u, v, inverse, below):
        self.lift = below * inverse
        self.east = jnp.maximum(u, 0.0) * inverse
        self.west = jnp.maximum(-u, 0.0) * inverse
        self.north = jnp.maximum(v, 0.0) * inverse
        self.south = jnp.maximum(-v, 0.0) * inverse
        self.centre = inverse - jnp.abs(u) * inverse - jnp.abs(v) * inverse

    def __call__(self, x, east, west, north, south):
        return (
            self.centre * x
            + self.east * east
            + self.west * west
            + self.north * north
            + self.south * south
        )


def shifted(x, east, west, north, south):
    lane, row = lanes_iota(), rows_iota()
    return (
        jnp.where(lane == 127, east, pltpu.roll(x, 127, 1)),
        jnp.where(lane == 0, west, pltpu.roll(x, 1, 1)),
        jnp.where(row == 7, north, pltpu.roll(x, 7, 0)),
        jnp.where(row == 0, south, pltpu.roll(x, 1, 0)),
    )


def first_kernel(
    field_ref,
    surface_ref,
    u_ref,
    v_ref,
    k_ref,
    inverse_ref,
    forcing_ref,
    low_ref,
    high_ref,
    west_ref,
    east_ref,
    out_ref,
    up_ref,
    down_ref,
):
    levels = k_ref.shape[0] // 8
    tracers = field_ref.shape[0] // (8 * levels)
    zero = jnp.zeros((8, 128), F32)
    east = [east_ref[t] for t in range(tracers)]
    west = [west_ref[t] for t in range(tracers)]

    def forward(g, carry):
        below, state = carry[0], list(carry[1])
        for j in range(GROUP):
            level = g * GROUP + j
            spot = pl.ds(level * 8, 8)
            advect = Advection(u_ref[spot, :], v_ref[spot, :], inverse_ref[spot, :], below)
            for t in range(tracers):
                at = t * levels + level
                x = field_ref[pl.ds(at * 8, 8), :]
                if j == 0:
                    x = x + jnp.where(g == 0, surface_ref[t], 0.0)
                around = shifted(
                    x,
                    pltpu.roll(east[t], 127 - level, 1),
                    pltpu.roll(west[t], 128 - level, 1),
                    high_ref[pl.ds(at, 1), :],
                    low_ref[pl.ds(at, 1), :],
                )
                state[t] = advect(x, *around) + advect.lift * state[t]
                out_ref[pl.ds(at * 8, 8), :] = state[t]
            below = k_ref[spot, :]
        return below, tuple(state)

    lax.fori_loop(0, levels // GROUP, forward, (zero, (zero,) * tracers))
    back(levels, tracers, k_ref, inverse_ref, out_ref, (), forcing_ref)
    count = tracers * levels
    lane, row = lanes_iota(), rows_iota()
    for ref, near, far in ((up_ref, 7, 6), (down_ref, 0, 1)):
        ref[0:count, :] = out_ref[pl.ds(near, count, stride=8), :]
        ref[count : 2 * count, :] = out_ref[pl.ds(far, count, stride=8), :]
        for at, source in ((2 * count, 126), (2 * count + 8, 0)):
            ref[at : at + 8, :] = zero
            for part in range((levels + 15) // 16):
                total = zero
                for start in range(16 * part, min(16 * part + 16, levels), 8):
                    for t in range(tracers):
                        x = ref[t * levels + start : t * levels + start + 8, :]
                        target = start % 16 * 8 + 2 * t
                        x = pltpu.roll(
                            x, (target - source + 128) % 128, 1, stride=8, stride_axis=0
                        )
                        total = jnp.where((lane - target - 8 * row) >> 1 == 0, x, total)
                ref[at + part : at + part + 1, :] = jnp.sum(total, axis=0, keepdims=True)


def back(levels, tracers, k_ref, inverse_ref, out_ref, others, added_ref=None):
    zero = jnp.zeros((8, 128), F32)

    def group(g, state):
        state = list(state)
        for j in range(GROUP):
            level = levels - 1 - g * GROUP - j
            spot = pl.ds(level * 8, 8)
            upper = k_ref[spot, :] * inverse_ref[spot, :]
            for t in range(tracers):
                here = pl.ds((t * levels + level) * 8, 8)
                state[t] = out_ref[here, :] + upper * state[t]
                if added_ref is None:
                    out_ref[here, :] = state[t]
                else:
                    out_ref[here, :] = state[t] + added_ref[here, :]
            for i, (ref, k, inverse) in enumerate(others):
                i += tracers
                state[i] = ref[spot, :] + k[spot, :] * inverse[spot, :] * state[i]
                ref[spot, :] = state[i]
        return tuple(state)

    lax.fori_loop(0, levels // GROUP, group, (zero,) * (tracers + len(others)))


def ring_kernel(
    low_ref, high_ref, west_ref, east_ref, u_ref, v_ref, k_ref, inverse_ref, *column_refs
):
    column_u_ref, column_v_ref, column_k_ref, column_inverse_ref = column_refs
    levels = u_ref.shape[0] // 8
    tracers = (low_ref.shape[0] - 3 * levels) // levels
    above = rows_iota() < tracers
    lane = lanes_iota()
    even = (lane & 1) == 0
    east = [east_ref[tracers + i] for i in range(3)]
    west = [west_ref[tracers + i] for i in range(3)]
    zero = jnp.zeros((8, 128), F32)
    column_u_ref[...] = jnp.zeros_like(column_u_ref)
    column_v_ref[...] = jnp.zeros_like(column_v_ref)
    below, inverse, column_below, column_inverse = zero, zero, zero, zero
    for level in range(levels):
        spot = pl.ds(level * 8, 8)
        at = [tracers * levels + i * levels + level for i in range(3)]
        u, v, k = (
            jnp.where(above, high_ref[pl.ds(i, 1), :], low_ref[pl.ds(i, 1), :]) for i in at
        )
        u_ref[spot, :] = u
        v_ref[spot, :] = jnp.where(above, v, -v)
        k_ref[spot, :] = k
        inverse = 1.0 / (1.0 + below + k - below * below * inverse)
        inverse_ref[spot, :] = inverse
        below = k
        u, v, k = (
            jnp.where(
                even,
                jnp.broadcast_to(e[:, level : level + 1], (8, 128)),
                jnp.broadcast_to(w[:, level : level + 1], (8, 128)),
            )
            for e, w in zip(east, west)
        )
        column_k_ref[spot, :] = k
        column_inverse = 1.0 / (1.0 + column_below + k - column_below * column_below * column_inverse)
        column_inverse_ref[spot, :] = column_inverse
        column_below = k
        packed = pl.ds(level // 16 * 8, 8)
        here = (lane >> 3) == level % 16
        column_u_ref[packed, :] = jnp.where(here, jnp.where(even, u, -u), column_u_ref[packed, :])
        column_v_ref[packed, :] = jnp.where(here, v, column_v_ref[packed, :])


def forcing_kernel(received_ref, out_ref):
    sources = received_ref.shape[0]
    levels = 72
    tracers = out_ref.shape[0] // (8 * levels)
    count = tracers * levels
    rows = jnp.concatenate([received_ref[s, 0:levels, :] for s in range(sources)], axis=1)
    rows = rows.astype(F32)
    tail = jnp.concatenate([received_ref[s, 64:80, :] for s in range(sources)], axis=1).astype(F32)
    high, low = [], []
    for t in range(tracers):
        product = rows * tail[8 + t : 9 + t, :]
        high.append(product.astype(BF16))
        low.append((product - high[t].astype(F32)).astype(BF16))
    products = jnp.concatenate(high + low, axis=0)
    cell_row = tail[12:13, :]
    cell_lane = tail[13:14, :].astype(BF16)
    lane = lax.broadcasted_iota(jnp.int32, (128, sources * 128), 0).astype(F32).astype(BF16)
    hot = jnp.where(lane == cell_lane, jnp.ones((), BF16), jnp.zeros((), BF16))
    for r in range(0, 8, 2):
        cells = jnp.concatenate(
            [hot * jnp.where(cell_row == r + i, 1.0, 0.0).astype(BF16) for i in range(2)], axis=0
        )
        both = lax.dot_general(
            products, cells, (((1,), (1,)), ((), ())), preferred_element_type=F32
        )
        both = both[:count] + both[count:]
        for i in range(2):
            out_ref[pl.ds(r + i, count, stride=8), :] = both[:, i * 128 : (i + 1) * 128]


def columns_kernel(field_ref, east_ref, west_ref):
    levels = 72
    tracers = field_ref.shape[0] // (8 * levels)
    for part in range(east_ref.shape[0] // 8):
        east = jnp.zeros((8, 128), F32)
        west = jnp.zeros((8, 128), F32)
        for level in range(16 * part, min(16 * part + 16, levels)):
            for t in range(tracers):
                x = field_ref[pl.ds((t * levels + level) * 8, 8), :]
                target = level % 16 * 8 + 2 * t
                east = add_column(east, x, 126, target, 2)
                west = add_column(west, x, 0, target, 2)
        east_ref[part * 8 : part * 8 + 8, :] = east
        west_ref[part * 8 : part * 8 + 8, :] = west


def relay_kernel(low_ref, high_ref, east_ref, west_ref, east_out, west_out):
    rows = east_ref.shape[0]
    corner = low_ref.shape[0] - 16
    for out, ref, at in ((east_out, east_ref, corner), (west_out, west_ref, corner + 8)):
        out[0:rows, :] = ref[...]
        out[rows : rows + 8, :] = high_ref[at : at + 8, :]
        out[rows + 8 : rows + 16, :] = low_ref[at : at + 8, :]


def last_kernel(
    field_ref,
    u_ref,
    v_ref,
    k_ref,
    inverse_ref,
    low_ref,
    high_ref,
    west_ref,
    east_ref,
    own_west_ref,
    own_east_ref,
    ring_u_ref,
    ring_v_ref,
    ring_k_ref,
    ring_inverse_ref,
    column_u_ref,
    column_v_ref,
    column_k_ref,
    column_inverse_ref,
    out_ref,
    middle_ref,
    near_ref,
    far_ref,
    inner_ref,
    ring_ref,
    packed_ref,
    column_ref,
):
    levels = k_ref.shape[0] // 8
    tracers = field_ref.shape[0] // (8 * levels)
    count = tracers * levels
    parts = own_east_ref.shape[0] // 8
    lane, row = lanes_iota(), rows_iota()
    even = (lane & 1) == 0
    above = row < tracers
    zero = jnp.zeros((8, 128), F32)
    for t in range(tracers):
        for side, (ref, edge) in enumerate(((high_ref, 7), (low_ref, 0))):
            spot = pl.ds(side * tracers + t, levels, stride=8)
            at = t * levels
            near_ref[spot, :] = ref[at : at + levels, :]
            far_ref[spot, :] = ref[count + at : count + at + levels, :]
            inner_ref[spot, :] = field_ref[pl.ds(at * 8 + edge, levels, stride=8), :]
    for part in range(parts):
        spot = pl.ds(part * 8, 8)
        east, west = east_ref[spot, :], west_ref[spot, :]
        x = jnp.where(even, east, west)
        outer = jnp.where(even, pltpu.roll(east, 127, 1), pltpu.roll(west, 1, 1))
        inner = jnp.where(
            even, pltpu.roll(own_east_ref[spot, :], 127, 1), pltpu.roll(own_west_ref[spot, :], 1, 1)
        )
        ends = [
            jnp.where(
                even,
                jnp.broadcast_to(east_ref[pl.ds(at, 1), :], (8, 128)),
                jnp.broadcast_to(west_ref[pl.ds(at, 1), :], (8, 128)),
            )
            for at in (parts * 8 + part, parts * 8 + 8 + part)
        ]
        north = jnp.where(row == 7, ends[0], pltpu.roll(x, 7, 0))
        south = jnp.where(row == 0, ends[1], pltpu.roll(x, 1, 0))
        advect = Advection(column_u_ref[spot, :], column_v_ref[spot, :], zero + 1.0, zero)
        packed_ref[spot, :] = advect(x, outer, inner, north, south)

    def forward(g, carry):
        below, ring_below, column_below = carry[0]
        state = list(carry[1])
        part = g * GROUP // 16
        east = east_ref[pl.ds(part * 8, 8), :]
        west = west_ref[pl.ds(part * 8, 8), :]
        corner_east, corner_west = (
            jnp.where(
                above,
                jnp.broadcast_to(ref[pl.ds(parts * 8 + part, 1), :], (8, 128)),
                jnp.broadcast_to(ref[pl.ds(parts * 8 + 8 + part, 1), :], (8, 128)),
            )
            for ref in (east_ref, west_ref)
        )
        packed = packed_ref[pl.ds(part * 8, 8), :]
        for j in range(GROUP):
            level = g * GROUP + j
            start = (level % 16) * 8
            spot = pl.ds(level * 8, 8)
            advect = Advection(u_ref[spot, :], v_ref[spot, :], inverse_ref[spot, :], below)
            for t in range(tracers):
                here = pl.ds((t * levels + level) * 8, 8)
                x = field_ref[here, :]
                around = shifted(
                    x,
                    pltpu.roll(east, 127 - start - 2 * t, 1),
                    pltpu.roll(west, 127 - start - 2 * t, 1),
                    near_ref[pl.ds(level * 8 + t, 1), :],
                    near_ref[pl.ds(level * 8 + tracers + t, 1), :],
                )
                state[t] = advect(x, *around) + advect.lift * state[t]
                middle_ref[here, :] = state[t]
            x = near_ref[spot, :]
            mine = start + 2 * (row % tracers)
            end_east = jnp.sum(jnp.where(lane == mine, corner_east, 0.0), axis=1, keepdims=True)
            end_west = jnp.sum(jnp.where(lane == mine + 1, corner_west, 0.0), axis=1, keepdims=True)
            advect = Advection(
                ring_u_ref[spot, :], ring_v_ref[spot, :], ring_inverse_ref[spot, :], ring_below
            )
            state[tracers] = (
                advect(
                    x,
                    jnp.where(lane == 127, end_east, pltpu.roll(x, 127, 1)),
                    jnp.where(lane == 0, end_west, pltpu.roll(x, 1, 1)),
                    far_ref[spot, :],
                    inner_ref[spot, :],
                )
                + advect.lift * state[tracers]
            )
            ring_ref[spot, :] = state[tracers]
            column_inverse = column_inverse_ref[spot, :]
            state[tracers + 1] = (
                pltpu.roll(packed, 128 - start, 1) * column_inverse
                + column_below * column_inverse * state[tracers + 1]
            )
            column_ref[spot, :] = state[tracers + 1]
            below, ring_below, column_below = (
                k_ref[spot, :],
                ring_k_ref[spot, :],
                column_k_ref[spot, :],
            )
        return (below, ring_below, column_below), tuple(state)

    lax.fori_loop(
        0, levels // GROUP, forward, ((zero, zero, zero), (zero,) * (tracers + 2))
    )
    back(
        levels,
        tracers,
        k_ref,
        inverse_ref,
        middle_ref,
        (
            (ring_ref, ring_k_ref, ring_inverse_ref),
            (column_ref, column_k_ref, column_inverse_ref),
        ),
    )

    def final(g, carry):
        below, state = carry[0], list(carry[1])
        for j in range(GROUP):
            level = g * GROUP + j
            spot = pl.ds(level * 8, 8)
            advect = Advection(u_ref[spot, :], v_ref[spot, :], inverse_ref[spot, :], below)
            sides = column_ref[spot, :]
            for t in range(tracers):
                here = pl.ds((t * levels + level) * 8, 8)
                x = middle_ref[here, :]
                around = shifted(
                    x,
                    pltpu.roll(sides, 127 - 2 * t, 1),
                    pltpu.roll(sides, 127 - 2 * t, 1),
                    ring_ref[pl.ds(level * 8 + t, 1), :],
                    ring_ref[pl.ds(level * 8 + tracers + t, 1), :],
                )
                state[t] = advect(x, *around) + advect.lift * state[t]
                out_ref[here, :] = state[t]
            below = k_ref[spot, :]
        return below, tuple(state)

    lax.fori_loop(0, levels // GROUP, final, (zero, (zero,) * tracers))
    back(levels, tracers, k_ref, inverse_ref, out_ref, ())


def to_rows(up, down):
    lat = lax.axis_size("lat")
    north = [(i, i + 1) for i in range(lat - 1)]
    return lax.ppermute(up, "lat", north), lax.ppermute(down, "lat", [(b, a) for a, b in north])


def to_columns(east, west):
    lon = lax.axis_size("lon")
    right = [(i, (i + 1) % lon) for i in range(lon)]
    return lax.ppermute(east, "lon", right), lax.ppermute(west, "lon", [(b, a) for a, b in right])


def body(
    adjoint_in,
    wind_u,
    wind_v,
    diffusion,
    kernel_rows,
    retrieval_misfit,
    retrieval_columns,
    retrieval_counts,
    station_cells,
    station_misfit,
):
    tracers, levels, lat_rows, lon_cells = adjoint_in.shape
    slots = kernel_rows.shape[1]
    tiles = lax.axis_size("lon")
    parts = (levels + 15) // 16
    full = jax.ShapeDtypeStruct((tracers * levels * 8, 128), F32)
    planes = jax.ShapeDtypeStruct((levels * 8, 128), F32)
    rows_one = jax.ShapeDtypeStruct(((tracers + 3) * levels, 128), F32)
    columns_one = jax.ShapeDtypeStruct((tracers + 3, 8, 128), F32)
    rows_two = jax.ShapeDtypeStruct((2 * tracers * levels + 16, 128), F32)
    columns_two = jax.ShapeDtypeStruct((parts * 8, 128), F32)
    columns_sent = jax.ShapeDtypeStruct((parts * 8 + 16, 128), F32)

    packed = pl.pallas_call(
        pack_kernel,
        out_shape=jax.ShapeDtypeStruct((tiles, 80, 128), BF16),
        in_specs=[pl.BlockSpec(memory_space=pltpu.SMEM)]
        + [pl.BlockSpec(memory_space=pltpu.VMEM)] * 3,
        compiler_params=pltpu.CompilerParams(vmem_limit_bytes=56 << 20),
        name="pack",
    )(retrieval_counts, kernel_rows, retrieval_misfit, retrieval_columns.reshape(slots // 128, 128))
    received = lax.all_to_all(packed, "lon", split_axis=0, concat_axis=0, tiled=True)

    field = adjoint_in.reshape(full.shape)
    u = wind_u.reshape(planes.shape)
    v = wind_v.reshape(planes.shape)
    k = diffusion.reshape(planes.shape)
    surface, up, down, east, west = vmem_call(
        prep_kernel,
        out_shape=(
            jax.ShapeDtypeStruct((tracers, 8, 128), F32),
            rows_one,
            rows_one,
            columns_one,
            columns_one,
        ),
        smem=2,
        name="prep",
    )(station_cells, station_misfit, field, u, v, k)
    low, high = to_rows(up, down)
    from_west, from_east = to_columns(east, west)
    inverse = vmem_call(factor_kernel, out_shape=planes, name="factor")(k)
    ring = vmem_call(
        ring_kernel,
        out_shape=(planes,) * 4 + (columns_two,) * 2 + (planes,) * 2,
        name="ring",
    )(low, high, from_west, from_east)
    forcing = vmem_call(forcing_kernel, out_shape=full, limit=30, name="forcing")(received)
    injected, up, down = vmem_call(
        first_kernel, out_shape=(full, rows_two, rows_two), name="first"
    )(field, surface, u, v, k, inverse, forcing, low, high, from_west, from_east)
    east, west = vmem_call(columns_kernel, out_shape=(columns_two,) * 2, name="columns")(injected)
    low, high = to_rows(up, down)
    sent = vmem_call(relay_kernel, out_shape=(columns_sent,) * 2, name="relay")(
        low, high, east, west
    )
    from_west, from_east = to_columns(*sent)
    last = vmem_call(
        last_kernel,
        out_shape=full,
        scratch=(full,) + (planes,) * 4 + (columns_two, planes),
        name="last",
    )(injected, u, v, k, inverse, low, high, from_west, from_east, west, east, *ring)
    return last.reshape(adjoint_in.shape)


def solution(mesh):
    return jax.shard_map(
        body,
        mesh=mesh,
        in_specs=(
            P(None, None, "lat", "lon"),
            P(None, "lat", "lon"),
            P(None, "lat", "lon"),
            P(None, "lat", "lon"),
            P(None, ("lat", "lon")),
            P(None, ("lat", "lon")),
            P(("lat", "lon")),
            P(("lat", "lon")),
            P(("lat", "lon")),
            P(None, ("lat", "lon")),
        ),
        out_specs=P(None, None, "lat", "lon"),
        check_vma=False,
    )
```

time: 114 us -> 82.2 us (0.72)
  the two profiles are of different devices: /device:TPU:230 before, /device:TPU:25 now
where the time goes in v1:
time: 82.2 us; the launch traced here: 81.7 us
  starting transfers between devices  45.3 us (55%)
  Pallas kernels  27.5 us (33%)
  waiting for transfers between devices  6.75 us (8%)
  local copies, waits for them, and re-layouts  1.04 us (1%)
  between operations  1.04 us (1%)
    pallas_call x8, Pallas kernels, run(): pl.pallas_call(kernel, out_shape=outs if is_tuple else outs[0], in_specs=...  22.3 us
    all_to_all x1, starting transfers between devices, body(): lax.all_to_all(packed, 'lon', split_axis=0, concat_axis=0, tiled=True)  12.9 us
    ppermute x2, starting transfers between devices, to_columns(): lax.ppermute(west, 'lon', [(b, a) for a, b in right])  11.4 us
    ppermute x2, starting transfers between devices, to_rows(): lax.ppermute(up, 'lat', north)  11.2 us
    ppermute x2, starting transfers between devices, to_columns(): lax.ppermute(east, 'lon', right)  5.96 us
    ppermute x2, waiting for transfers between devices, to_rows(): lax.ppermute(down, 'lat', [(b, a) for a, b in north])  5.61 us
    pallas_call x1, Pallas kernels, body(): pl.pallas_call(pack_kernel, out_shape=jax.ShapeDtypeStruct((tiles, 80, 12...  5.25 us
    ppermute x2, starting transfers between devices, to_rows(): lax.ppermute(down, 'lat', [(b, a) for a, b in north])  3.84 us
  transfers between devices with their start and end apart: 9, of which 2 were waited for; matrix products, arithmetic and copies ran while one was open for 0% of the time, Pallas kernels for 13%

profile of v1, /device:TPU:25, one launch (start us, length us, event | category | flops | bytes accessed | tf_op | source)
XLA Modules:
  0.0 81.7 jit_solution(15236800422709436968)
XLA Ops:
  0.0 0.0 copy-start.4
  0.0 0.0 copy-start.5
  0.0 0.0 copy-start
  0.0 0.0 copy-start.3
  0.0 0.0 copy-start.2
  0.0 0.0 copy-start.1
  0.8 5.3 %pack.1 = bf16[32,80,128]{2,1,0:T(8,128)(2,1)} custom-call(s32[1]{0:T(128)S(6)} %copy.12.count_ref, bf16[72,2048]{1,0:T(8,128)(2,1)} %rows_ref.1, bf16[4,2048]{1,0:T(4,128)(2,1)} %misfit_ref.1, s32[16,128]{1,0:T(8,128)} %bitcast.19), custom_call_target="tpu_custom_call" | custom-call | tf_op jit(solution)/shard_map/pack/pallas_call | solution.py:614
  6.1 12.9 %all-to-all-start = ((bf16[32,80,128]{2,1,0:T(8,128)(2,1)}), bf16[32,80,128]{2,1,0:T(8,128)(2,1)S(1)}, u32[]{:S(2)}, u32[]{:S(2)}) async-start(bf16[32,80,128]{2,1,0:T(8,128)(2,1)} %pack.1), calls=%async_computation | async-start | bytes 1310720 | tf_op jit(solution)/shard_map/all_to_all | solution.py:622
  19.0 0.0 copy-done.4
  19.0 0.0 copy-done.5
  19.0 0.0 copy-done
  19.0 0.0 copy-done.3
  19.0 0.0 copy-done.2
  19.0 0.0 copy-done.1
  19.0 3.2 %prep.1 = (f32[4,8,128]{2,1,0:T(8,128)S(1)}, f32[504,128]{1,0:T(8,128)}, f32[504,128]{1,0:T(8,128)}, f32[7,8,128]{2,1,0:T(8,128)}, f32[7,8,128]{2,1,0:T(8,128)}) custom-call(s32[16]{0:T(128)S(1)} %copy-done.5, f32[4,16]{1,0:T(4,128)S(1)} %copy-done.4, f32[2304,128]{1,0:T(8,128)S(1)} %bitcast.11, f32[576,128]{1,0:T(8,128)S(1)} %bitcast.13, ...), custom_call_target="tpu_custom_call" | custom-call | tf_op jit(solution)/shard_map/prep/pallas_call | solution.py:24
  22.2 5.2 %collective-permute-start = (f32[504,128]{1,0:T(8,128)}, f32[504,128]{1,0:T(8,128)S(1)}, u32[]{:S(2)}, u32[]{:S(2)}) collective-permute-start(f32[504,128]{1,0:T(8,128)} %get-tuple-element.26), channel_id=1, source_target_pairs={{0,32},{32,64},{64,96},{96,128},{128,160},{160,192},{192,224},{224... | collective-permute-start | bytes 774152 | tf_op jit(solution)/shard_map/ppermute | solution.py:581
  27.4 1.9 %collective-permute-start.1 = (f32[504,128]{1,0:T(8,128)}, f32[504,128]{1,0:T(8,128)S(1)}, u32[]{:S(2)}, u32[]{:S(2)}) collective-permute-start(f32[504,128]{1,0:T(8,128)} %get-tuple-element.27), channel_id=1, source_target_pairs={{32,0},{64,32},{96,64},{128,96},{160,128},{192,160},{224,192},{256... | collective-permute-start | bytes 774152 | tf_op jit(solution)/shard_map/ppermute | solution.py:581
  29.4 3.4 %collective-permute-start.2 = (f32[7,8,128]{2,1,0:T(8,128)}, f32[7,8,128]{2,1,0:T(8,128)}, u32[]{:S(2)}, u32[]{:S(2)}) collective-permute-start(f32[7,8,128]{2,1,0:T(8,128)} %get-tuple-element.28), channel_id=1, source_target_pairs={{0,1},{1,2},{2,3},{3,4},{4,5},{5,6},{6,7},{7,8},{8,9},{9,10},{10,1... | collective-permute-start | bytes 86024 | tf_op jit(solution)/shard_map/ppermute | solution.py:587
  32.8 5.3 %collective-permute-start.3 = (f32[7,8,128]{2,1,0:T(8,128)}, f32[7,8,128]{2,1,0:T(8,128)}, u32[]{:S(2)}, u32[]{:S(2)}) collective-permute-start(f32[7,8,128]{2,1,0:T(8,128)} %get-tuple-element.29), channel_id=1, source_target_pairs={{1,0},{2,1},{3,2},{4,3},{5,4},{6,5},{7,6},{8,7},{9,8},{10,9},{11,1... | collective-permute-start | bytes 86024 | tf_op jit(solution)/shard_map/ppermute | solution.py:587
  38.1 0.6 factor.1.inverse_ref
  38.7 0.0 all-to-all-done.received_ref
  38.7 5.1 %forcing.1.forcing_ref = f32[2304,128]{1,0:T(8,128)S(1)} custom-call(bf16[32,80,128]{2,1,0:T(8,128)(2,1)S(1)} %all-to-all-done.received_ref), custom_call_target="tpu_custom_call" | custom-call | tf_op jit(solution)/shard_map/forcing/pallas_call | solution.py:24
  43.8 0.0 collective-permute-done.2.west_ref
  43.8 0.0 collective-permute-done.3.east_ref
  43.9 0.0 collective-permute-done.low_ref
  43.9 0.0 collective-permute-done.1.high_ref
  43.9 4.0 %first.1 = (f32[2304,128]{1,0:T(8,128)S(1)}, f32[592,128]{1,0:T(8,128)S(1)}, f32[592,128]{1,0:T(8,128)S(1)}) custom-call(f32[2304,128]{1,0:T(8,128)S(1)} %bitcast.12, f32[4,8,128]{2,1,0:T(8,128)S(1)} %get-tuple-element.25.surface_ref, f32[576,128]{1,0:T(8,128)S(1)} %bitcast.14, f32[576,128]{1,0:T(8,128)S(1)} %bitcast.17, f32[576,128]{1,0:T(8,128)S(1)} %bitcast.9, ...), custom_call_target="tpu_custom_call" | custom-call | tf_op jit(solution)/shard_map/first/pallas_call | solution.py:24
  47.9 6.0 %collective-permute-start.4 = (f32[592,128]{1,0:T(8,128)S(1)}, f32[592,128]{1,0:T(8,128)S(1)}, u32[]{:S(2)}, u32[]{:S(2)}) collective-permute-start(f32[592,128]{1,0:T(8,128)S(1)} %get-tuple-element.31), channel_id=1, source_target_pairs={{0,32},{32,64},{64,96},{96,128},{128,160},{160,192},{192,224},{224... | collective-permute-start | bytes 909320 | tf_op jit(solution)/shard_map/ppermute | solution.py:581
  53.9 1.9 %collective-permute-start.5 = (f32[592,128]{1,0:T(8,128)S(1)}, f32[592,128]{1,0:T(8,128)S(1)}, u32[]{:S(2)}, u32[]{:S(2)}) collective-permute-start(f32[592,128]{1,0:T(8,128)S(1)} %get-tuple-element.32), channel_id=1, source_target_pairs={{32,0},{64,32},{96,64},{128,96},{160,128},{192,160},{224,192},{256... | collective-permute-start | bytes 909320 | tf_op jit(solution)/shard_map/ppermute | solution.py:581
  55.9 0.7 columns.1
  56.5 1.1 %collective-permute-done.4.low_ref = f32[592,128]{1,0:T(8,128)S(1)} collective-permute-done((f32[592,128]{1,0:T(8,128)S(1)}, f32[592,128]{1,0:T(8,128)S(1)}, u32[]{:S(2)}, u32[]{:S(2)}) %collective-permute-start.4) | collective-permute-done | bytes 303136 | tf_op jit(solution)/shard_map/ppermute | solution.py:581
  57.7 5.6 %collective-permute-done.5.high_ref = f32[592,128]{1,0:T(8,128)S(1)} collective-permute-done((f32[592,128]{1,0:T(8,128)S(1)}, f32[592,128]{1,0:T(8,128)S(1)}, u32[]{:S(2)}, u32[]{:S(2)}) %collective-permute-start.5) | collective-permute-done | bytes 303136 | tf_op jit(solution)/shard_map/ppermute | solution.py:581
  63.3 2.5 %collective-permute-start.6 = (f32[56,128]{1,0:T(8,128)S(1)}, f32[56,128]{1,0:T(8,128)S(1)}, u32[]{:S(2)}, u32[]{:S(2)}) collective-permute-start(f32[56,128]{1,0:T(8,128)S(1)} %get-tuple-element.35), channel_id=1, source_target_pairs={{0,1},{1,2},{2,3},{3,4},{4,5},{5,6},{6,7},{7,8},{8,9},{9,10},{10,1... | collective-permute-start | bytes 86024 | tf_op jit(solution)/shard_map/ppermute | solution.py:587
  65.8 6.0 %collective-permute-start.7 = (f32[56,128]{1,0:T(8,128)S(1)}, f32[56,128]{1,0:T(8,128)S(1)}, u32[]{:S(2)}, u32[]{:S(2)}) collective-permute-start(f32[56,128]{1,0:T(8,128)S(1)} %get-tuple-element.36), channel_id=1, source_target_pairs={{1,0},{2,1},{3,2},{4,3},{5,4},{6,5},{7,6},{8,7},{9,8},{10,9},{11,1... | collective-permute-start | bytes 86024 | tf_op jit(solution)/shard_map/ppermute | solution.py:587
  71.9 1.4 %ring.1 = (f32[576,128]{1,0:T(8,128)S(1)}, f32[576,128]{1,0:T(8,128)S(1)}, f32[576,128]{1,0:T(8,128)S(1)}, f32[576,128]{1,0:T(8,128)S(1)}, f32[40,128]{1,0:T(8,1...) custom-call(f32[504,128]{1,0:T(8,128)S(1)} %collective-permute-done.low_ref, ...), custom_call_target="tpu_custom_call" | custom-call | tf_op jit(solution)/shard_map/ring/pallas_call | solution.py:24
  73.3 0.0 collective-permute-done.6.west_ref
  73.3 0.0 collective-permute-done.7.east_ref
  73.4 7.3 %last.1 = f32[2304,128]{1,0:T(8,128)S(1)} custom-call(f32[2304,128]{1,0:T(8,128)S(1)} %get-tuple-element.30.field_ref, f32[576,128]{1,0:T(8,128)S(1)} %bitcast.15, f32[576,128]{1,0:T(8,128)S(1)} %bitcast.18, f32[576,128]{1,0:T(8,128)S(1)} %bitcast.10, f32[576,128]{1,0:T(8,128)S(1)} %factor.1.inverse_ref, f32[592,128]{1,0:T(8,128)S(1)} %collective-permute-done.4.low_ref, ...), custom_call_target="tpu_custom_call" | custom-call | tf_op jit(solution)/shard_map/last/pallas_call | solution.py:24
  80.7 1.0 %copy.11 = f32[4,72,8,128]{3,2,1,0:T(8,128)} copy(f32[4,72,8,128]{3,2,1,0:T(8,128)S(1)} %bitcast.6) | data formatting | bytes 2359296
  (1 shorter events, 0.0 us)
Async XLA Ops:
  0.0 19.0 %copy-start.4 = (f32[4,16]{1,0:T(4,128)S(1)}, f32[4,16]{1,0:T(4,128)}, u32[]{:S(2)}) copy-start(f32[4,16]{1,0:T(4,128)} %weights_ref.1) | copy-start | bytes 772
  0.0 19.0 %copy-start.5 = (s32[16]{0:T(128)S(1)}, s32[16]{0:T(128)}, u32[]{:S(2)}) copy-start(s32[16]{0:T(128)} %cells_ref.1) | copy-start | bytes 196
  0.0 19.0 %copy-start = (f32[72,8,128]{2,1,0:T(8,128)S(1)}, f32[72,8,128]{2,1,0:T(8,128)}, u32[]{:S(2)}) copy-start(f32[72,8,128]{2,1,0:T(8,128)} %param.13) | copy-start | bytes 884740
  0.0 19.0 %copy-start.3 = (f32[72,8,128]{2,1,0:T(8,128)S(1)}, f32[72,8,128]{2,1,0:T(8,128)}, u32[]{:S(2)}) copy-start(f32[72,8,128]{2,1,0:T(8,128)} %param.12) | copy-start | bytes 884740
  0.0 19.0 %copy-start.2 = (f32[72,8,128]{2,1,0:T(8,128)S(1)}, f32[72,8,128]{2,1,0:T(8,128)}, u32[]{:S(2)}) copy-start(f32[72,8,128]{2,1,0:T(8,128)} %param.11) | copy-start | bytes 884740
  0.0 19.0 %copy-start.1 = (f32[4,72,8,128]{3,2,1,0:T(8,128)S(1)}, f32[4,72,8,128]{3,2,1,0:T(8,128)}, u32[]{:S(2)}) copy-start(f32[4,72,8,128]{3,2,1,0:T(8,128)} %param.10) | copy-start | bytes 3538948
  6.1 32.6 %all-to-all-start = ((bf16[32,80,128]{2,1,0:T(8,128)(2,1)}), bf16[32,80,128]{2,1,0:T(8,128)(2,1)S(1)}, u32[]{:S(2)}, u32[]{:S(2)}) async-start(bf16[32,80,128]{2,1,0:T(8,128)(2,1)} %pack.1), calls=%async_computation | async-start | bytes 1310720 | tf_op jit(solution)/shard_map/all_to_all | solution.py:622
  22.2 21.7 %collective-permute-start = (f32[504,128]{1,0:T(8,128)}, f32[504,128]{1,0:T(8,128)S(1)}, u32[]{:S(2)}, u32[]{:S(2)}) collective-permute-start(f32[504,128]{1,0:T(8,128)} %get-tuple-element.26), channel_id=1, source_target_pairs={{0,32},{32,64},{64,96},{96,128},{128,160},{160,192},{192,224},{224... | collective-permute-start | bytes 774152 | tf_op jit(solution)/shard_map/ppermute | solution.py:581
  27.4 16.4 %collective-permute-start.1 = (f32[504,128]{1,0:T(8,128)}, f32[504,128]{1,0:T(8,128)S(1)}, u32[]{:S(2)}, u32[]{:S(2)}) collective-permute-start(f32[504,128]{1,0:T(8,128)} %get-tuple-element.27), channel_id=1, source_target_pairs={{32,0},{64,32},{96,64},{128,96},{160,128},{192,160},{224,192},{256... | collective-permute-start | bytes 774152 | tf_op jit(solution)/shard_map/ppermute | solution.py:581
  29.4 14.5 %collective-permute-start.2 = (f32[7,8,128]{2,1,0:T(8,128)}, f32[7,8,128]{2,1,0:T(8,128)}, u32[]{:S(2)}, u32[]{:S(2)}) collective-permute-start(f32[7,8,128]{2,1,0:T(8,128)} %get-tuple-element.28), channel_id=1, source_target_pairs={{0,1},{1,2},{2,3},{3,4},{4,5},{5,6},{6,7},{7,8},{8,9},{9,10},{10,1... | collective-permute-start | bytes 86024 | tf_op jit(solution)/shard_map/ppermute | solution.py:587
  32.8 11.1 %collective-permute-start.3 = (f32[7,8,128]{2,1,0:T(8,128)}, f32[7,8,128]{2,1,0:T(8,128)}, u32[]{:S(2)}, u32[]{:S(2)}) collective-permute-start(f32[7,8,128]{2,1,0:T(8,128)} %get-tuple-element.29), channel_id=1, source_target_pairs={{1,0},{2,1},{3,2},{4,3},{5,4},{6,5},{7,6},{8,7},{9,8},{10,9},{11,1... | collective-permute-start | bytes 86024 | tf_op jit(solution)/shard_map/ppermute | solution.py:587
  47.9 9.7 %collective-permute-start.4 = (f32[592,128]{1,0:T(8,128)S(1)}, f32[592,128]{1,0:T(8,128)S(1)}, u32[]{:S(2)}, u32[]{:S(2)}) collective-permute-start(f32[592,128]{1,0:T(8,128)S(1)} %get-tuple-element.31), channel_id=1, source_target_pairs={{0,32},{32,64},{64,96},{96,128},{128,160},{160,192},{192,224},{224... | collective-permute-start | bytes 909320 | tf_op jit(solution)/shard_map/ppermute | solution.py:581
  53.9 9.3 %collective-permute-start.5 = (f32[592,128]{1,0:T(8,128)S(1)}, f32[592,128]{1,0:T(8,128)S(1)}, u32[]{:S(2)}, u32[]{:S(2)}) collective-permute-start(f32[592,128]{1,0:T(8,128)S(1)} %get-tuple-element.32), channel_id=1, source_target_pairs={{32,0},{64,32},{96,64},{128,96},{160,128},{192,160},{224,192},{256... | collective-permute-start | bytes 909320 | tf_op jit(solution)/shard_map/ppermute | solution.py:581
  63.3 10.1 %collective-permute-start.6 = (f32[56,128]{1,0:T(8,128)S(1)}, f32[56,128]{1,0:T(8,128)S(1)}, u32[]{:S(2)}, u32[]{:S(2)}) collective-permute-start(f32[56,128]{1,0:T(8,128)S(1)} %get-tuple-element.35), channel_id=1, source_target_pairs={{0,1},{1,2},{2,3},{3,4},{4,5},{5,6},{6,7},{7,8},{8,9},{9,10},{10,1... | collective-permute-start | bytes 86024 | tf_op jit(solution)/shard_map/ppermute | solution.py:587
  65.8 7.5 %collective-permute-start.7 = (f32[56,128]{1,0:T(8,128)S(1)}, f32[56,128]{1,0:T(8,128)S(1)}, u32[]{:S(2)}, u32[]{:S(2)}) collective-permute-start(f32[56,128]{1,0:T(8,128)S(1)} %get-tuple-element.36), channel_id=1, source_target_pairs={{1,0},{2,1},{3,2},{4,3},{5,4},{6,5},{7,6},{8,7},{9,8},{10,9},{11,1... | collective-permute-start | bytes 86024 | tf_op jit(solution)/shard_map/ppermute | solution.py:587

commit v2 on v1

--- a/solution.py
+++ b/solution.py
@@ -7,7 +7,7 @@
 
 F32 = jnp.float32
 BF16 = jnp.bfloat16
-GROUP = 8
+GROUP = 72
 
 
 def vmem_call(kernel, *, out_shape, smem=0, scratch=(), limit=16, name):
@@ -117,6 +117,7 @@
 
 
 def prep_kernel(
+    odd_ref,
     cells_ref,
     weights_ref,
     field_ref,
@@ -124,10 +125,10 @@
     v_ref,
     k_ref,
     surface_ref,
-    up_ref,
-    down_ref,
-    east_ref,
-    west_ref,
+    rows_one_ref,
+    rows_two_ref,
+    columns_one_ref,
+    columns_two_ref,
 ):
     levels = k_ref.shape[0] // 8
     tracers = field_ref.shape[0] // (8 * levels)
@@ -140,14 +141,20 @@
         surface.append(total)
         surface_ref[t] = total
     count = tracers * levels
-    for row, ref in ((7, up_ref), (0, down_ref)):
-        ref[0:count, :] = field_ref[pl.ds(row, count, stride=8), :]
-        for t in range(tracers):
-            top = slice(t * levels, t * levels + 1)
-            ref[top, :] = ref[top, :] + surface[t][row : row + 1, :]
-        for i, plane in enumerate((u_ref, v_ref, k_ref)):
-            at = count + i * levels
-            ref[at : at + levels, :] = plane[pl.ds(row, levels, stride=8), :]
+    odd_row, odd_column = odd_ref[0] == 1, odd_ref[1] == 1
+
+    def send(spot, values):
+        rows_one_ref[spot, :] = jnp.where(odd_row, values[1], values[0])
+        rows_two_ref[spot, :] = jnp.where(odd_row, values[0], values[1])
+
+    send(slice(0, count), [field_ref[pl.ds(row, count, stride=8), :] for row in (7, 0)])
+    for t in range(tracers):
+        top = pl.ds(t * levels * 8, 8)
+        total = field_ref[top, :] + surface[t]
+        send(slice(t * levels, t * levels + 1), [total[row : row + 1, :] for row in (7, 0)])
+    for i, plane in enumerate((u_ref, v_ref, k_ref)):
+        at = count + i * levels
+        send(slice(at, at + levels), [plane[pl.ds(row, levels, stride=8), :] for row in (7, 0)])
 
     def group(g, carry):
         east, west = list(carry[0]), list(carry[1])
@@ -166,8 +173,8 @@
     zeros = (jnp.zeros((8, 128), F32),) * (tracers + 3)
     east, west = lax.fori_loop(0, levels // GROUP, group, (zeros, zeros))
     for i in range(tracers + 3):
-        east_ref[i] = east[i]
-        west_ref[i] = west[i]
+        columns_one_ref[i] = jnp.where(odd_column, west[i], east[i])
+        columns_two_ref[i] = jnp.where(odd_column, east[i], west[i])
 
 
 def factor_kernel(k_ref, inverse_ref):
@@ -215,26 +222,26 @@
 
 
 def first_kernel(
+    odd_ref,
     field_ref,
     surface_ref,
     u_ref,
     v_ref,
     k_ref,
     inverse_ref,
-    forcing_ref,
-    low_ref,
-    high_ref,
-    west_ref,
-    east_ref,
+    rows_one_ref,
+    rows_two_ref,
+    columns_one_ref,
+    columns_two_ref,
     out_ref,
-    up_ref,
-    down_ref,
 ):
     levels = k_ref.shape[0] // 8
     tracers = field_ref.shape[0] // (8 * levels)
     zero = jnp.zeros((8, 128), F32)
-    east = [east_ref[t] for t in range(tracers)]
-    west = [west_ref[t] for t in range(tracers)]
+    odd_row, odd_column = odd_ref[0] == 1, odd_ref[1] == 1
+    both = [(columns_one_ref[t], columns_two_ref[t]) for t in range(tracers)]
+    east = [jnp.where(odd_column, two, one) for one, two in both]
+    west = [jnp.where(odd_column, one, two) for one, two in both]
 
     def forward(g, carry):
         below, state = carry[0], list(carry[1])
@@ -247,12 +254,13 @@
                 x = field_ref[pl.ds(at * 8, 8), :]
                 if j == 0:
                     x = x + jnp.where(g == 0, surface_ref[t], 0.0)
+                one, two = rows_one_ref[pl.ds(at, 1), :], rows_two_ref[pl.ds(at, 1), :]
                 around = shifted(
                     x,
                     pltpu.roll(east[t], 127 - level, 1),
                     pltpu.roll(west[t], 128 - level, 1),
-                    high_ref[pl.ds(at, 1), :],
-                    low_ref[pl.ds(at, 1), :],
+                    jnp.where(odd_row, two, one),
+                    jnp.where(odd_row, one, two),
                 )
                 state[t] = advect(x, *around) + advect.lift * state[t]
                 out_ref[pl.ds(at * 8, 8), :] = state[t]
@@ -260,28 +268,10 @@
         return below, tuple(state)
 
     lax.fori_loop(0, levels // GROUP, forward, (zero, (zero,) * tracers))
-    back(levels, tracers, k_ref, inverse_ref, out_ref, (), forcing_ref)
-    count = tracers * levels
-    lane, row = lanes_iota(), rows_iota()
-    for ref, near, far in ((up_ref, 7, 6), (down_ref, 0, 1)):
-        ref[0:count, :] = out_ref[pl.ds(near, count, stride=8), :]
-        ref[count : 2 * count, :] = out_ref[pl.ds(far, count, stride=8), :]
-        for at, source in ((2 * count, 126), (2 * count + 8, 0)):
-            ref[at : at + 8, :] = zero
-            for part in range((levels + 15) // 16):
-                total = zero
-                for start in range(16 * part, min(16 * part + 16, levels), 8):
-                    for t in range(tracers):
-                        x = ref[t * levels + start : t * levels + start + 8, :]
-                        target = start % 16 * 8 + 2 * t
-                        x = pltpu.roll(
-                            x, (target - source + 128) % 128, 1, stride=8, stride_axis=0
-                        )
-                        total = jnp.where((lane - target - 8 * row) >> 1 == 0, x, total)
-                ref[at + part : at + part + 1, :] = jnp.sum(total, axis=0, keepdims=True)
-
-
-def back(levels, tracers, k_ref, inverse_ref, out_ref, others, added_ref=None):
+    back(levels, tracers, k_ref, inverse_ref, out_ref, ())
+
+
+def back(levels, tracers, k_ref, inverse_ref, out_ref, others):
     zero = jnp.zeros((8, 128), F32)
 
     def group(g, state):
@@ -293,10 +283,7 @@
             for t in range(tracers):
                 here = pl.ds((t * levels + level) * 8, 8)
                 state[t] = out_ref[here, :] + upper * state[t]
-                if added_ref is None:
-                    out_ref[here, :] = state[t]
-                else:
-                    out_ref[here, :] = state[t] + added_ref[here, :]
+                out_ref[here, :] = state[t]
             for i, (ref, k, inverse) in enumerate(others):
                 i += tracers
                 state[i] = ref[spot, :] + k[spot, :] * inverse[spot, :] * state[i]
@@ -307,16 +294,28 @@
 
 
 def ring_kernel(
-    low_ref, high_ref, west_ref, east_ref, u_ref, v_ref, k_ref, inverse_ref, *column_refs
+    odd_ref,
+    rows_one_ref,
+    rows_two_ref,
+    columns_one_ref,
+    columns_two_ref,
+    u_ref,
+    v_ref,
+    k_ref,
+    inverse_ref,
+    *column_refs,
 ):
     column_u_ref, column_v_ref, column_k_ref, column_inverse_ref = column_refs
     levels = u_ref.shape[0] // 8
-    tracers = (low_ref.shape[0] - 3 * levels) // levels
+    tracers = (rows_one_ref.shape[0] - 3 * levels) // levels
     above = rows_iota() < tracers
+    from_one = above ^ (odd_ref[0] == 1)
     lane = lanes_iota()
     even = (lane & 1) == 0
-    east = [east_ref[tracers + i] for i in range(3)]
-    west = [west_ref[tracers + i] for i in range(3)]
+    odd_column = odd_ref[1] == 1
+    both = [(columns_one_ref[tracers + i], columns_two_ref[tracers + i]) for i in range(3)]
+    east = [jnp.where(odd_column, two, one) for one, two in both]
+    west = [jnp.where(odd_column, one, two) for one, two in both]
     zero = jnp.zeros((8, 128), F32)
     column_u_ref[...] = jnp.zeros_like(column_u_ref)
     column_v_ref[...] = jnp.zeros_like(column_v_ref)
@@ -325,7 +324,8 @@
         spot = pl.ds(level * 8, 8)
         at = [tracers * levels + i * levels + level for i in range(3)]
         u, v, k = (
-            jnp.where(above, high_ref[pl.ds(i, 1), :], low_ref[pl.ds(i, 1), :]) for i in at
+            jnp.where(from_one, rows_one_ref[pl.ds(i, 1), :], rows_two_ref[pl.ds(i, 1), :])
+            for i in at
         )
         u_ref[spot, :] = u
         v_ref[spot, :] = jnp.where(above, v, -v)
@@ -351,10 +351,9 @@
         column_v_ref[packed, :] = jnp.where(here, v, column_v_ref[packed, :])
 
 
-def forcing_kernel(received_ref, out_ref):
+def forcing_rows(received_ref, pairs):
     sources = received_ref.shape[0]
-    levels = 72
-    tracers = out_ref.shape[0] // (8 * levels)
+    levels, tracers = 72, 4
     count = tracers * levels
     rows = jnp.concatenate([received_ref[s, 0:levels, :] for s in range(sources)], axis=1)
     rows = rows.astype(F32)
@@ -369,27 +368,70 @@
     cell_lane = tail[13:14, :].astype(BF16)
     lane = lax.broadcasted_iota(jnp.int32, (128, sources * 128), 0).astype(F32).astype(BF16)
     hot = jnp.where(lane == cell_lane, jnp.ones((), BF16), jnp.zeros((), BF16))
-    for r in range(0, 8, 2):
+    for pair in pairs:
         cells = jnp.concatenate(
-            [hot * jnp.where(cell_row == r + i, 1.0, 0.0).astype(BF16) for i in range(2)], axis=0
+            [hot * jnp.where(cell_row == r, 1.0, 0.0).astype(BF16) for r in pair], axis=0
         )
         both = lax.dot_general(
             products, cells, (((1,), (1,)), ((), ())), preferred_element_type=F32
         )
-        both = both[:count] + both[count:]
-        for i in range(2):
-            out_ref[pl.ds(r + i, count, stride=8), :] = both[:, i * 128 : (i + 1) * 128]
-
-
-def columns_kernel(field_ref, east_ref, west_ref):
+        yield both[:count] + both[count:]
+
+
+EDGE_ROWS = ((0, 7), (1, 6))
+INNER_ROWS = ((2, 3), (4, 5))
+
+
+def edge_kernel(odd_ref, received_ref, first_ref, edge_ref, sent_one_ref, sent_two_ref):
+    count = edge_ref.shape[1]
     levels = 72
-    tracers = field_ref.shape[0] // (8 * levels)
+    tracers = count // levels
+    lane, row = lanes_iota(), rows_iota()
+    zero = jnp.zeros((8, 128), F32)
+    odd_row = odd_ref[0] == 1
+    for at, (pair, both) in enumerate(zip(EDGE_ROWS, forcing_rows(received_ref, EDGE_ROWS))):
+        down, up = (
+            first_ref[pl.ds(r, count, stride=8), :] + both[:, i * 128 : (i + 1) * 128]
+            for i, r in enumerate(pair)
+        )
+        edge_ref[2 * at] = down
+        edge_ref[2 * at + 1] = up
+        spot = slice(at * count, (at + 1) * count)
+        sent_one_ref[spot, :] = jnp.where(odd_row, down, up)
+        sent_two_ref[spot, :] = jnp.where(odd_row, up, down)
+    for ref in (sent_one_ref, sent_two_ref):
+        for at, source in ((2 * count, 126), (2 * count + 8, 0)):
+            ref[at : at + 8, :] = zero
+            for part in range((levels + 15) // 16):
+                total = zero
+                for start in range(16 * part, min(16 * part + 16, levels), 8):
+                    for t in range(tracers):
+                        x = ref[t * levels + start : t * levels + start + 8, :]
+                        target = start % 16 * 8 + 2 * t
+                        x = pltpu.roll(
+                            x, (target - source + 128) % 128, 1, stride=8, stride_axis=0
+                        )
+                        total = jnp.where((lane - target - 8 * row) >> 1 == 0, x, total)
+                ref[at + part : at + part + 1, :] = jnp.sum(total, axis=0, keepdims=True)
+
+
+def inner_kernel(received_ref, first_ref, edge_ref, out_ref, east_ref, west_ref):
+    count = edge_ref.shape[1]
+    levels = 72
+    tracers = count // levels
+    for at, pair in enumerate(EDGE_ROWS):
+        for i, r in enumerate(pair):
+            out_ref[pl.ds(r, count, stride=8), :] = edge_ref[2 * at + i]
+    for pair, both in zip(INNER_ROWS, forcing_rows(received_ref, INNER_ROWS)):
+        for i, r in enumerate(pair):
+            spot = pl.ds(r, count, stride=8)
+            out_ref[spot, :] = first_ref[spot, :] + both[:, i * 128 : (i + 1) * 128]
     for part in range(east_ref.shape[0] // 8):
         east = jnp.zeros((8, 128), F32)
         west = jnp.zeros((8, 128), F32)
         for level in range(16 * part, min(16 * part + 16, levels)):
             for t in range(tracers):
-                x = field_ref[pl.ds((t * levels + level) * 8, 8), :]
+                x = out_ref[pl.ds((t * levels + level) * 8, 8), :]
                 target = level % 16 * 8 + 2 * t
                 east = add_column(east, x, 126, target, 2)
                 west = add_column(west, x, 0, target, 2)
@@ -397,25 +439,32 @@
         west_ref[part * 8 : part * 8 + 8, :] = west
 
 
-def relay_kernel(low_ref, high_ref, east_ref, west_ref, east_out, west_out):
+def relay_kernel(odd_ref, one_ref, two_ref, east_ref, west_ref, sent_one_ref, sent_two_ref):
     rows = east_ref.shape[0]
-    corner = low_ref.shape[0] - 16
-    for out, ref, at in ((east_out, east_ref, corner), (west_out, west_ref, corner + 8)):
-        out[0:rows, :] = ref[...]
-        out[rows : rows + 8, :] = high_ref[at : at + 8, :]
-        out[rows + 8 : rows + 16, :] = low_ref[at : at + 8, :]
+    corner = one_ref.shape[0] - 16
+    odd_row, odd_column = odd_ref[0] == 1, odd_ref[1] == 1
+
+    def send(spot, values):
+        sent_one_ref[spot, :] = jnp.where(odd_column, values[1], values[0])
+        sent_two_ref[spot, :] = jnp.where(odd_column, values[0], values[1])
+
+    send(slice(0, rows), [east_ref[...], west_ref[...]])
+    ends = [[ref[at : at + 8, :] for at in (corner, corner + 8)] for ref in (one_ref, two_ref)]
+    for at, side in ((rows, ~odd_row), (rows + 8, odd_row)):
+        send(slice(at, at + 8), [jnp.where(side, one, two) for one, two in zip(*ends)])
 
 
 def last_kernel(
+    odd_ref,
     field_ref,
     u_ref,
     v_ref,
     k_ref,
     inverse_ref,
-    low_ref,
-    high_ref,
-    west_ref,
-    east_ref,
+    rows_one_ref,
+    rows_two_ref,
+    columns_one_ref,
+    columns_two_ref,
     own_west_ref,
     own_east_ref,
     ring_u_ref,
@@ -434,6 +483,7 @@
     ring_ref,
     packed_ref,
     column_ref,
+    sides_ref,
 ):
     levels = k_ref.shape[0] // 8
     tracers = field_ref.shape[0] // (8 * levels)
@@ -443,16 +493,20 @@
     even = (lane & 1) == 0
     above = row < tracers
     zero = jnp.zeros((8, 128), F32)
+    odd_row, odd_column = odd_ref[0] == 1, odd_ref[1] == 1
+    sides_ref[0] = jnp.where(odd_column, columns_two_ref[...], columns_one_ref[...])
+    sides_ref[1] = jnp.where(odd_column, columns_one_ref[...], columns_two_ref[...])
     for t in range(tracers):
-        for side, (ref, edge) in enumerate(((high_ref, 7), (low_ref, 0))):
+        for side, (swap, edge) in enumerate(((odd_row, 7), (~odd_row, 0))):
             spot = pl.ds(side * tracers + t, levels, stride=8)
             at = t * levels
-            near_ref[spot, :] = ref[at : at + levels, :]
-            far_ref[spot, :] = ref[count + at : count + at + levels, :]
+            for ref, start in ((near_ref, at), (far_ref, count + at)):
+                rows = slice(start, start + levels)
+                ref[spot, :] = jnp.where(swap, rows_two_ref[rows, :], rows_one_ref[rows, :])
             inner_ref[spot, :] = field_ref[pl.ds(at * 8 + edge, levels, stride=8), :]
     for part in range(parts):
         spot = pl.ds(part * 8, 8)
-        east, west = east_ref[spot, :], west_ref[spot, :]
+        east, west = sides_ref[0, spot, :], sides_ref[1, spot, :]
         x = jnp.where(even, east, west)
         outer = jnp.where(even, pltpu.roll(east, 127, 1), pltpu.roll(west, 1, 1))
         inner = jnp.where(
@@ -461,8 +515,8 @@
         ends = [
             jnp.where(
                 even,
-                jnp.broadcast_to(east_ref[pl.ds(at, 1), :], (8, 128)),
-                jnp.broadcast_to(west_ref[pl.ds(at, 1), :], (8, 128)),
+                jnp.broadcast_to(sides_ref[0, pl.ds(at, 1), :], (8, 128)),
+                jnp.broadcast_to(sides_ref[1, pl.ds(at, 1), :], (8, 128)),
             )
             for at in (parts * 8 + part, parts * 8 + 8 + part)
         ]
@@ -474,21 +528,21 @@
     def forward(g, carry):
         below, ring_below, column_below = carry[0]
         state = list(carry[1])
-        part = g * GROUP // 16
-        east = east_ref[pl.ds(part * 8, 8), :]
-        west = west_ref[pl.ds(part * 8, 8), :]
-        corner_east, corner_west = (
-            jnp.where(
-                above,
-                jnp.broadcast_to(ref[pl.ds(parts * 8 + part, 1), :], (8, 128)),
-                jnp.broadcast_to(ref[pl.ds(parts * 8 + 8 + part, 1), :], (8, 128)),
-            )
-            for ref in (east_ref, west_ref)
-        )
-        packed = packed_ref[pl.ds(part * 8, 8), :]
         for j in range(GROUP):
             level = g * GROUP + j
             start = (level % 16) * 8
+            part = level // 16
+            packed = packed_ref[pl.ds(part * 8, 8), :]
+            east = sides_ref[0, pl.ds(part * 8, 8), :]
+            west = sides_ref[1, pl.ds(part * 8, 8), :]
+            corner_east, corner_west = (
+                jnp.where(
+                    above,
+                    jnp.broadcast_to(sides_ref[i, pl.ds(parts * 8 + part, 1), :], (8, 128)),
+                    jnp.broadcast_to(sides_ref[i, pl.ds(parts * 8 + 8 + part, 1), :], (8, 128)),
+                )
+                for i in range(2)
+            )
             spot = pl.ds(level * 8, 8)
             advect = Advection(u_ref[spot, :], v_ref[spot, :], inverse_ref[spot, :], below)
             for t in range(tracers):
@@ -575,16 +629,11 @@
     back(levels, tracers, k_ref, inverse_ref, out_ref, ())
 
 
-def to_rows(up, down):
-    lat = lax.axis_size("lat")
-    north = [(i, i + 1) for i in range(lat - 1)]
-    return lax.ppermute(up, "lat", north), lax.ppermute(down, "lat", [(b, a) for a, b in north])
-
-
-def to_columns(east, west):
-    lon = lax.axis_size("lon")
-    right = [(i, (i + 1) % lon) for i in range(lon)]
-    return lax.ppermute(east, "lon", right), lax.ppermute(west, "lon", [(b, a) for a, b in right])
+def swap(one, two, axis, periodic):
+    size = lax.axis_size(axis)
+    pairs = [(i, (i + 1) % size) for i in range(size if periodic else size - 1)]
+    both = [[(a, b) for p in pairs[start::2] for a, b in (p, p[::-1])] for start in (0, 1)]
+    return lax.ppermute(one, axis, both[0]), lax.ppermute(two, axis, both[1])
 
 
 def body(
@@ -625,7 +674,8 @@
     u = wind_u.reshape(planes.shape)
     v = wind_v.reshape(planes.shape)
     k = diffusion.reshape(planes.shape)
-    surface, up, down, east, west = vmem_call(
+    odd = jnp.stack([lax.axis_index("lat") & 1, lax.axis_index("lon") & 1])
+    surface, *sent = vmem_call(
         prep_kernel,
         out_shape=(
             jax.ShapeDtypeStruct((tracers, 8, 128), F32),
@@ -634,33 +684,48 @@
             columns_one,
             columns_one,
         ),
-        smem=2,
+        smem=3,
         name="prep",
-    )(station_cells, station_misfit, field, u, v, k)
-    low, high = to_rows(up, down)
-    from_west, from_east = to_columns(east, west)
+    )(odd, station_cells, station_misfit, field, u, v, k)
+    edges = swap(*sent[:2], "lat", False) + swap(*sent[2:], "lon", True)
     inverse = vmem_call(factor_kernel, out_shape=planes, name="factor")(k)
     ring = vmem_call(
         ring_kernel,
         out_shape=(planes,) * 4 + (columns_two,) * 2 + (planes,) * 2,
+        smem=1,
         name="ring",
-    )(low, high, from_west, from_east)
-    forcing = vmem_call(forcing_kernel, out_shape=full, limit=30, name="forcing")(received)
-    injected, up, down = vmem_call(
-        first_kernel, out_shape=(full, rows_two, rows_two), name="first"
-    )(field, surface, u, v, k, inverse, forcing, low, high, from_west, from_east)
-    east, west = vmem_call(columns_kernel, out_shape=(columns_two,) * 2, name="columns")(injected)
-    low, high = to_rows(up, down)
-    sent = vmem_call(relay_kernel, out_shape=(columns_sent,) * 2, name="relay")(
-        low, high, east, west
+    )(odd, *edges)
+    first = vmem_call(first_kernel, out_shape=full, smem=1, name="first")(
+        odd, field, surface, u, v, k, inverse, *edges
     )
-    from_west, from_east = to_columns(*sent)
+    edge, *sent = vmem_call(
+        edge_kernel,
+        out_shape=(
+            jax.ShapeDtypeStruct((4, tracers * levels, 128), F32),
+            rows_two,
+            rows_two,
+        ),
+        smem=1,
+        limit=30,
+        name="edge",
+    )(odd, received, first)
+    injected, east, west = vmem_call(
+        inner_kernel, out_shape=(full, columns_two, columns_two), limit=30, name="inner"
+    )(received, first, edge)
+    rows = swap(*sent, "lat", False)
+    sent = vmem_call(relay_kernel, out_shape=(columns_sent,) * 2, smem=1, name="relay")(
+        odd, *rows, east, west
+    )
+    columns = swap(*sent, "lon", True)
     last = vmem_call(
         last_kernel,
         out_shape=full,
-        scratch=(full,) + (planes,) * 4 + (columns_two, planes),
+        smem=1,
+        scratch=(full,)
+        + (planes,) * 4
+        + (columns_two, planes, jax.ShapeDtypeStruct((2,) + columns_sent.shape, F32)),
         name="last",
-    )(injected, u, v, k, inverse, low, high, from_west, from_east, west, east, *ring)
+    )(odd, injected, u, v, k, inverse, *rows, *columns, west, east, *ring)
     return last.reshape(adjoint_in.shape)
 
 

time: 82.2 us -> 76.7 us (0.933)
  the two profiles are of different devices: /device:TPU:25 before, /device:TPU:32 now
where the time goes in v2:
time: 76.7 us; the launch traced here: 76.3 us
  starting transfers between devices  40.1 us (52%)
  Pallas kernels  24.3 us (32%)
  waiting for transfers between devices  7.47 us (10%)
  local copies, waits for them, and re-layouts  3.19 us (4%)
  between operations  1.1 us (1%)
    ppermute x8, starting transfers between devices, swap(): return (lax.ppermute(one, axis, both[0]), lax.ppermute(two, axis, both[1]))  27 us
    pallas_call x8, Pallas kernels, run(): pl.pallas_call(kernel, out_shape=outs if is_tuple else outs[0], in_specs=...  19.1 us
    all_to_all x1, starting transfers between devices, body(): lax.all_to_all(packed, 'lon', split_axis=0, concat_axis=0, tiled=True)  13.2 us
    ppermute x8, waiting for transfers between devices, swap(): return (lax.ppermute(one, axis, both[0]), lax.ppermute(two, axis, both[1]))  7.47 us
    pallas_call x1, Pallas kernels, body(): pl.pallas_call(pack_kernel, out_shape=jax.ShapeDtypeStruct((tiles, 80, 12...  5.26 us
    unnamed x33, local copies, waits for them, and re-layouts  3.19 us
  transfers between devices with their start and end apart: 9, of which 3 were waited for; matrix products, arithmetic and copies ran while one was open for 0% of the time, Pallas kernels for 12%

profile of v2, /device:TPU:32, one launch (start us, length us, event | category | flops | bytes accessed | tf_op | source)
XLA Modules:
  0.0 76.3 jit_solution(15859859945542623179)
XLA Ops:
  0.0 0.0 copy-start.5
  0.0 0.0 copy-start.2
  0.0 0.0 copy-start.1
  0.8 5.3 %pack.1 = bf16[32,80,128]{2,1,0:T(8,128)(2,1)} custom-call(s32[1]{0:T(128)S(6)} %copy.12.count_ref, bf16[72,2048]{1,0:T(8,128)(2,1)} %rows_ref.1, bf16[4,2048]{1,0:T(4,128)(2,1)} %misfit_ref.1, s32[16,128]{1,0:T(8,128)} %bitcast.21), custom_call_target="tpu_custom_call" | custom-call | tf_op jit(solution)/shard_map/pack/pallas_call | solution.py:663
  6.1 13.2 %all-to-all-start = ((bf16[32,80,128]{2,1,0:T(8,128)(2,1)}), bf16[32,80,128]{2,1,0:T(8,128)(2,1)S(1)}, u32[]{:S(2)}, u32[]{:S(2)}) async-start(bf16[32,80,128]{2,1,0:T(8,128)(2,1)} %pack.1), calls=%async_computation | async-start | bytes 1310720 | tf_op jit(solution)/shard_map/all_to_all | solution.py:671
  19.3 0.1 pad_add_fusion.odd_ref
  19.3 0.0 copy-done.14
  19.4 0.0 copy-done.15
  19.4 0.0 copy-done
  19.4 0.0 copy-done.5
  19.4 0.0 copy-done.2
  19.4 0.0 copy-done.1
  19.4 0.0 copy-start.3
  19.4 0.0 copy-start.6
  19.4 1.9 %prep.1 = (f32[4,8,128]{2,1,0:T(8,128)S(1)}, f32[504,128]{1,0:T(8,128)S(1)}, f32[504,128]{1,0:T(8,128)S(1)}, f32[7,8,128]{2,1,0:T(8,128)S(1)}, f32[7,8,128]{2,1,0:T(8,128)S(1)}) custom-call(s32[2]{0:T(128)S(1)} %pad_add_fusion.odd_ref, s32[16]{0:T(128)S(1)} %copy-done.15, f32[4,16]{1,0:T(4,128)S(1)} %copy-done.14, f32[2304,128]{1,0:T(8,128)S(1)} %bitcast.13, ...), custom_call_target="tpu_custom_call" | custom-call | tf_op jit(solution)/shard_map/prep/pallas_call | solution.py:24
  21.3 1.9 %collective-permute-start = (f32[504,128]{1,0:T(8,128)S(1)}, f32[504,128]{1,0:T(8,128)S(1)}, u32[]{:S(2)}, u32[]{:S(2)}) collective-permute-start(f32[504,128]{1,0:T(8,128)S(1)} %get-tuple-element.27), channel_id=1, source_target_pairs={{0,32},{32,0},{64,96},{96,64},{128,160},{160,128},{192,224},{224,1... | collective-permute-start | bytes 774152 | tf_op jit(solution)/shard_map/ppermute | solution.py:636
  23.2 2.5 %collective-permute-start.1 = (f32[504,128]{1,0:T(8,128)S(1)}, f32[504,128]{1,0:T(8,128)S(1)}, u32[]{:S(2)}, u32[]{:S(2)}) collective-permute-start(f32[504,128]{1,0:T(8,128)S(1)} %get-tuple-element.28), channel_id=1, source_target_pairs={{32,64},{64,32},{96,128},{128,96},{160,192},{192,160},{224,256},{2... | collective-permute-start | bytes 774152 | tf_op jit(solution)/shard_map/ppermute | solution.py:636
  25.7 3.7 %collective-permute-start.2 = (f32[7,8,128]{2,1,0:T(8,128)S(1)}, f32[7,8,128]{2,1,0:T(8,128)S(1)}, u32[]{:S(2)}, u32[]{:S(2)}) collective-permute-start(f32[7,8,128]{2,1,0:T(8,128)S(1)} %get-tuple-element.29), channel_id=1, source_target_pairs={{0,1},{1,0},{2,3},{3,2},{4,5},{5,4},{6,7},{7,6},{8,9},{9,8},{10,11... | collective-permute-start | bytes 86024 | tf_op jit(solution)/shard_map/ppermute | solution.py:636
  29.4 6.2 %collective-permute-start.3 = (f32[7,8,128]{2,1,0:T(8,128)S(1)}, f32[7,8,128]{2,1,0:T(8,128)S(1)}, u32[]{:S(2)}, u32[]{:S(2)}) collective-permute-start(f32[7,8,128]{2,1,0:T(8,128)S(1)} %get-tuple-element.30), channel_id=1, source_target_pairs={{1,2},{2,1},{3,4},{4,3},{5,6},{6,5},{7,8},{8,7},{9,10},{10,9},{11,... | collective-permute-start | bytes 86024 | tf_op jit(solution)/shard_map/ppermute | solution.py:636
  35.6 0.5 factor.1.inverse_ref
  36.1 0.0 collective-permute-done.2.columns_one_ref
  36.1 2.7 %collective-permute-done.3.columns_two_ref = f32[7,8,128]{2,1,0:T(8,128)S(1)} collective-permute-done((f32[7,8,128]{2,1,0:T(8,128)S(1)}, f32[7,8,128]{2,1,0:T(8,128)S(1)}, u32[]{:S(2)}, u32[]{:S(2)}) %collective-permute-start.3) | collective-permute-done | bytes 28704 | tf_op jit(solution)/shard_map/ppermute | solution.py:636
  38.8 0.0 collective-permute-done.rows_one_ref
  38.8 0.0 collective-permute-done.1.rows_two_ref
  38.8 0.0 copy-done.3
  38.8 0.0 copy-done.6
  38.8 2.3 %first.1.first_ref = f32[2304,128]{1,0:T(8,128)S(1)} custom-call(s32[2]{0:T(128)S(1)} %pad_add_fusion.odd_ref, f32[2304,128]{1,0:T(8,128)S(1)} %bitcast.14, f32[4,8,128]{2,1,0:T(8,128)S(1)} %get-tuple-element.26.surface_ref, f32[576,128]{1,0:T(8,128)S(1)} %bitcast.16, f32[576,128]{1,0:T(8,128)S(1)} %bitcast.19, f32[576,128]{1,0:T(8,128)S(1)} %bitcast.11, ...), custom_call_target="tpu_custom_call" | custom-call | tf_op jit(solution)/shard_map/first/pallas_call | solution.py:24
  41.1 0.0 copy-start.8
  41.1 0.7 copy-done.8
  41.8 0.7 copy-done.10
  42.5 0.7 copy-done.12
  43.2 0.0 all-to-all-done.received_ref
  43.2 3.4 %edge.1 = (f32[4,288,128]{2,1,0:T(8,128)S(1)}, f32[592,128]{1,0:T(8,128)S(1)}, f32[592,128]{1,0:T(8,128)S(1)}) custom-call(s32[2]{0:T(128)S(1)} %pad_add_fusion.odd_ref, bf16[32,80,128]{2,1,0:T(8,128)(2,1)S(1)} %all-to-all-done.received_ref, f32[2304,128]{1,0:T(8,128)S(1)} %first.1.first_ref), custom_call_target="tpu_custom_call" | custom-call | tf_op jit(solution)/shard_map/edge/pallas_call | solution.py:24
  46.6 1.9 %collective-permute-start.4 = (f32[592,128]{1,0:T(8,128)S(1)}, f32[592,128]{1,0:T(8,128)S(1)}, u32[]{:S(2)}, u32[]{:S(2)}) collective-permute-start(f32[592,128]{1,0:T(8,128)S(1)} %get-tuple-element.33), channel_id=1, source_target_pairs={{0,32},{32,0},{64,96},{96,64},{128,160},{160,128},{192,224},{224,1... | collective-permute-start | bytes 909320 | tf_op jit(solution)/shard_map/ppermute | solution.py:636
  48.5 3.0 %collective-permute-start.5 = (f32[592,128]{1,0:T(8,128)S(1)}, f32[592,128]{1,0:T(8,128)S(1)}, u32[]{:S(2)}, u32[]{:S(2)}) collective-permute-start(f32[592,128]{1,0:T(8,128)S(1)} %get-tuple-element.34), channel_id=1, source_target_pairs={{32,64},{64,32},{96,128},{128,96},{160,192},{192,160},{224,256},{2... | collective-permute-start | bytes 909320 | tf_op jit(solution)/shard_map/ppermute | solution.py:636
  51.6 3.4 %inner.1 = (f32[2304,128]{1,0:T(8,128)S(1)}, f32[40,128]{1,0:T(8,128)S(1)}, f32[40,128]{1,0:T(8,128)S(1)}) custom-call(bf16[32,80,128]{2,1,0:T(8,128)(2,1)S(1)} %all-to-all-done.received_ref, f32[2304,128]{1,0:T(8,128)S(1)} %first.1.first_ref, f32[4,288,128]{2,1,0:T(8,128)S(1)} %get-tuple-element.31.edge_ref), custom_call_target="tpu_custom_call" | custom-call | tf_op jit(solution)/shard_map/inner/pallas_call | solution.py:24
  55.0 0.0 copy-start.4
  55.0 0.0 copy-start.7
  55.0 0.0 collective-permute-done.4.one_ref.rows_one_ref
  55.0 2.8 %collective-permute-done.5.two_ref.rows_two_ref = f32[592,128]{1,0:T(8,128)S(1)} collective-permute-done((f32[592,128]{1,0:T(8,128)S(1)}, f32[592,128]{1,0:T(8,128)S(1)}, u32[]{:S(2)}, u32[]{:S(2)}) %collective-permute-start.5) | collective-permute-done | bytes 303136 | tf_op jit(solution)/shard_map/ppermute | solution.py:636
  57.9 0.6 relay.1
  58.4 1.9 %collective-permute-start.6 = (f32[56,128]{1,0:T(8,128)S(1)}, f32[56,128]{1,0:T(8,128)S(1)}, u32[]{:S(2)}, u32[]{:S(2)}) collective-permute-start(f32[56,128]{1,0:T(8,128)S(1)} %get-tuple-element.37), channel_id=1, source_target_pairs={{0,1},{1,0},{2,3},{3,2},{4,5},{5,4},{6,7},{7,6},{8,9},{9,8},{10,11... | collective-permute-start | bytes 86024 | tf_op jit(solution)/shard_map/ppermute | solution.py:636
  60.3 5.8 %collective-permute-start.7 = (f32[56,128]{1,0:T(8,128)S(1)}, f32[56,128]{1,0:T(8,128)S(1)}, u32[]{:S(2)}, u32[]{:S(2)}) collective-permute-start(f32[56,128]{1,0:T(8,128)S(1)} %get-tuple-element.38), channel_id=1, source_target_pairs={{1,2},{2,1},{3,4},{4,3},{5,6},{6,5},{7,8},{8,7},{9,10},{10,9},{11,... | collective-permute-start | bytes 86024 | tf_op jit(solution)/shard_map/ppermute | solution.py:636
  66.2 1.2 %ring.1 = (f32[576,128]{1,0:T(8,128)S(1)}, f32[576,128]{1,0:T(8,128)S(1)}, f32[576,128]{1,0:T(8,128)S(1)}, f32[576,128]{1,0:T(8,128)S(1)}, f32[40,128]{1,0:T(8,1...) custom-call(s32[2]{0:T(128)S(1)} %pad_add_fusion.odd_ref, ...), custom_call_target="tpu_custom_call" | custom-call | tf_op jit(solution)/shard_map/ring/pallas_call | solution.py:24
  67.5 0.0 collective-permute-done.6.columns_one_ref
  67.5 2.0 %collective-permute-done.7.columns_two_ref = f32[56,128]{1,0:T(8,128)S(1)} collective-permute-done((f32[56,128]{1,0:T(8,128)S(1)}, f32[56,128]{1,0:T(8,128)S(1)}, u32[]{:S(2)}, u32[]{:S(2)}) %collective-permute-start.7) | collective-permute-done | bytes 28704 | tf_op jit(solution)/shard_map/ppermute | solution.py:636
  69.4 5.9 %last.1 = f32[2304,128]{1,0:T(8,128)S(1)} custom-call(s32[2]{0:T(128)S(1)} %pad_add_fusion.odd_ref, f32[2304,128]{1,0:T(8,128)S(1)} %get-tuple-element.32.field_ref, f32[576,128]{1,0:T(8,128)S(1)} %bitcast.17, f32[576,128]{1,0:T(8,128)S(1)} %bitcast.20, f32[576,128]{1,0:T(8,128)S(1)} %bitcast.12, f32[576,128]{1,0:T(8,128)S(1)} %copy-done.9, ...), custom_call_target="tpu_custom_call" | custom-call | tf_op jit(solution)/shard_map/last/pallas_call | solution.py:24
  75.3 1.0 %copy.11 = f32[4,72,8,128]{3,2,1,0:T(8,128)} copy(f32[4,72,8,128]{3,2,1,0:T(8,128)S(1)} %bitcast.8) | data formatting | bytes 2359296
  (13 shorter events, 0.0 us)
Async XLA Ops:
  0.0 19.4 %copy-start.14 = (f32[4,16]{1,0:T(4,128)S(1)}, f32[4,16]{1,0:T(4,128)}, u32[]{:S(2)}) copy-start(f32[4,16]{1,0:T(4,128)} %weights_ref.1) | copy-start | bytes 772
  0.0 19.4 %copy-start.15 = (s32[16]{0:T(128)S(1)}, s32[16]{0:T(128)}, u32[]{:S(2)}) copy-start(s32[16]{0:T(128)} %cells_ref.1) | copy-start | bytes 196
  0.0 19.4 %copy-start = (f32[72,8,128]{2,1,0:T(8,128)S(1)}, f32[72,8,128]{2,1,0:T(8,128)}, u32[]{:S(2)}) copy-start(f32[72,8,128]{2,1,0:T(8,128)} %param.13) | copy-start | bytes 884740
  0.0 19.3 %copy-start.5 = (f32[72,8,128]{2,1,0:T(8,128)S(1)}, f32[72,8,128]{2,1,0:T(8,128)}, u32[]{:S(2)}) copy-start(f32[72,8,128]{2,1,0:T(8,128)} %param.12) | copy-start | bytes 884740
  0.0 19.3 %copy-start.2 = (f32[72,8,128]{2,1,0:T(8,128)S(1)}, f32[72,8,128]{2,1,0:T(8,128)}, u32[]{:S(2)}) copy-start(f32[72,8,128]{2,1,0:T(8,128)} %param.11) | copy-start | bytes 884740
  0.0 19.3 %copy-start.1 = (f32[4,72,8,128]{3,2,1,0:T(8,128)S(1)}, f32[4,72,8,128]{3,2,1,0:T(8,128)}, u32[]{:S(2)}) copy-start(f32[4,72,8,128]{3,2,1,0:T(8,128)} %param.10) | copy-start | bytes 3538948
  6.1 37.1 %all-to-all-start = ((bf16[32,80,128]{2,1,0:T(8,128)(2,1)}), bf16[32,80,128]{2,1,0:T(8,128)(2,1)S(1)}, u32[]{:S(2)}, u32[]{:S(2)}) async-start(bf16[32,80,128]{2,1,0:T(8,128)(2,1)} %pack.1), calls=%async_computation | async-start | bytes 1310720 | tf_op jit(solution)/shard_map/all_to_all | solution.py:671
  19.4 19.4 %copy-start.3 = (f32[72,8,128]{2,1,0:T(8,128)S(1)}, f32[72,8,128]{2,1,0:T(8,128)}, u32[]{:S(2)}) copy-start(f32[72,8,128]{2,1,0:T(8,128)} %param.11) | copy-start | bytes 884740
  19.4 19.4 %copy-start.6 = (f32[72,8,128]{2,1,0:T(8,128)S(1)}, f32[72,8,128]{2,1,0:T(8,128)}, u32[]{:S(2)}) copy-start(f32[72,8,128]{2,1,0:T(8,128)} %param.12) | copy-start | bytes 884740
  21.3 17.5 %collective-permute-start = (f32[504,128]{1,0:T(8,128)S(1)}, f32[504,128]{1,0:T(8,128)S(1)}, u32[]{:S(2)}, u32[]{:S(2)}) collective-permute-start(f32[504,128]{1,0:T(8,128)S(1)} %get-tuple-element.27), channel_id=1, source_target_pairs={{0,32},{32,0},{64,96},{96,64},{128,160},{160,128},{192,224},{224,1... | collective-permute-start | bytes 774152 | tf_op jit(solution)/shard_map/ppermute | solution.py:636
  23.2 15.6 %collective-permute-start.1 = (f32[504,128]{1,0:T(8,128)S(1)}, f32[504,128]{1,0:T(8,128)S(1)}, u32[]{:S(2)}, u32[]{:S(2)}) collective-permute-start(f32[504,128]{1,0:T(8,128)S(1)} %get-tuple-element.28), channel_id=1, source_target_pairs={{32,64},{64,32},{96,128},{128,96},{160,192},{192,160},{224,256},{2... | collective-permute-start | bytes 774152 | tf_op jit(solution)/shard_map/ppermute | solution.py:636
  25.7 10.4 %collective-permute-start.2 = (f32[7,8,128]{2,1,0:T(8,128)S(1)}, f32[7,8,128]{2,1,0:T(8,128)S(1)}, u32[]{:S(2)}, u32[]{:S(2)}) collective-permute-start(f32[7,8,128]{2,1,0:T(8,128)S(1)} %get-tuple-element.29), channel_id=1, source_target_pairs={{0,1},{1,0},{2,3},{3,2},{4,5},{5,4},{6,7},{7,6},{8,9},{9,8},{10,11... | collective-permute-start | bytes 86024 | tf_op jit(solution)/shard_map/ppermute | solution.py:636
  29.4 9.4 %collective-permute-start.3 = (f32[7,8,128]{2,1,0:T(8,128)S(1)}, f32[7,8,128]{2,1,0:T(8,128)S(1)}, u32[]{:S(2)}, u32[]{:S(2)}) collective-permute-start(f32[7,8,128]{2,1,0:T(8,128)S(1)} %get-tuple-element.30), channel_id=1, source_target_pairs={{1,2},{2,1},{3,4},{4,3},{5,6},{6,5},{7,8},{8,7},{9,10},{10,9},{11,... | collective-permute-start | bytes 86024 | tf_op jit(solution)/shard_map/ppermute | solution.py:636
  41.1 0.7 copy-start.8
  41.8 0.7 copy-start.10
  42.5 0.7 copy-start.12
  46.6 8.4 %collective-permute-start.4 = (f32[592,128]{1,0:T(8,128)S(1)}, f32[592,128]{1,0:T(8,128)S(1)}, u32[]{:S(2)}, u32[]{:S(2)}) collective-permute-start(f32[592,128]{1,0:T(8,128)S(1)} %get-tuple-element.33), channel_id=1, source_target_pairs={{0,32},{32,0},{64,96},{96,64},{128,160},{160,128},{192,224},{224,1... | collective-permute-start | bytes 909320 | tf_op jit(solution)/shard_map/ppermute | solution.py:636
  48.5 9.3 %collective-permute-start.5 = (f32[592,128]{1,0:T(8,128)S(1)}, f32[592,128]{1,0:T(8,128)S(1)}, u32[]{:S(2)}, u32[]{:S(2)}) collective-permute-start(f32[592,128]{1,0:T(8,128)S(1)} %get-tuple-element.34), channel_id=1, source_target_pairs={{32,64},{64,32},{96,128},{128,96},{160,192},{192,160},{224,256},{2... | collective-permute-start | bytes 909320 | tf_op jit(solution)/shard_map/ppermute | solution.py:636
  51.6 14.6 %copy-start.11 = (f32[504,128]{1,0:T(8,128)S(1)}, f32[504,128]{1,0:T(8,128)}, u32[]{:S(2)}) copy-start(f32[504,128]{1,0:T(8,128)} %copy-done.10) | copy-start | bytes 774148
  51.6 14.6 %copy-start.13 = (f32[504,128]{1,0:T(8,128)S(1)}, f32[504,128]{1,0:T(8,128)}, u32[]{:S(2)}) copy-start(f32[504,128]{1,0:T(8,128)} %copy-done.12) | copy-start | bytes 774148
  55.0 14.4 %copy-start.4 = (f32[72,8,128]{2,1,0:T(8,128)S(1)}, f32[72,8,128]{2,1,0:T(8,128)}, u32[]{:S(2)}) copy-start(f32[72,8,128]{2,1,0:T(8,128)} %param.11) | copy-start | bytes 884740
  55.0 14.4 %copy-start.7 = (f32[72,8,128]{2,1,0:T(8,128)S(1)}, f32[72,8,128]{2,1,0:T(8,128)}, u32[]{:S(2)}) copy-start(f32[72,8,128]{2,1,0:T(8,128)} %param.12) | copy-start | bytes 884740
  55.0 14.4 %copy-start.9 = (f32[576,128]{1,0:T(8,128)S(1)}, f32[576,128]{1,0:T(8,128)}, u32[]{:S(2)}) copy-start(f32[576,128]{1,0:T(8,128)} %copy-done.8) | copy-start | bytes 884740
  58.4 9.0 %collective-permute-start.6 = (f32[56,128]{1,0:T(8,128)S(1)}, f32[56,128]{1,0:T(8,128)S(1)}, u32[]{:S(2)}, u32[]{:S(2)}) collective-permute-start(f32[56,128]{1,0:T(8,128)S(1)} %get-tuple-element.37), channel_id=1, source_target_pairs={{0,1},{1,0},{2,3},{3,2},{4,5},{5,4},{6,7},{7,6},{8,9},{9,8},{10,11... | collective-permute-start | bytes 86024 | tf_op jit(solution)/shard_map/ppermute | solution.py:636
  60.3 9.1 %collective-permute-start.7 = (f32[56,128]{1,0:T(8,128)S(1)}, f32[56,128]{1,0:T(8,128)S(1)}, u32[]{:S(2)}, u32[]{:S(2)}) collective-permute-start(f32[56,128]{1,0:T(8,128)S(1)} %get-tuple-element.38), channel_id=1, source_target_pairs={{1,2},{2,1},{3,4},{4,3},{5,6},{6,5},{7,8},{8,7},{9,10},{10,9},{11,... | collective-permute-start | bytes 86024 | tf_op jit(solution)/shard_map/ppermute | solution.py:636

commit v3 on v2

--- a/solution.py
+++ b/solution.py
@@ -10,7 +10,7 @@
 GROUP = 72
 
 
-def vmem_call(kernel, *, out_shape, smem=0, scratch=(), limit=16, name):
+def vmem_call(kernel, *, out_shape, smem=0, scratch=(), copies=0, limit=16, name):
     is_tuple = isinstance(out_shape, tuple)
     outs = out_shape if is_tuple else (out_shape,)
     outs = tuple(pltpu.VMEM(o.shape, o.dtype) for o in outs)
@@ -21,11 +21,14 @@
         )
         specs = [pl.BlockSpec(memory_space=pltpu.SMEM)] * smem
         specs += [pl.BlockSpec(memory_space=pltpu.VMEM)] * (len(args) - smem)
+        own = {"out_specs": pl.BlockSpec(memory_space=pl.ANY)} if copies else {}
         return pl.pallas_call(
             kernel,
-            out_shape=outs if is_tuple else outs[0],
+            out_shape=out_shape if copies else outs if is_tuple else outs[0],
             in_specs=specs,
-            scratch_shapes=[pltpu.VMEM(o.shape, o.dtype) for o in scratch],
+            scratch_shapes=[pltpu.VMEM(o.shape, o.dtype) for o in scratch]
+            + [pltpu.SemaphoreType.DMA((copies,))] * (copies > 0),
+            **own,
             compiler_params=pltpu.CompilerParams(vmem_limit_bytes=limit << 20),
             name=name,
         )(*args)
@@ -44,7 +47,7 @@
 def pack_kernel(count_ref, rows_ref, misfit_ref, columns_ref, out_ref):
     chunks = columns_ref.shape[0]
     tiles = out_ref.shape[0]
-    count = count_ref[0]
+    count = count_ref[...]
     lane = lax.broadcasted_iota(jnp.int32, (1, 128), 1)
     tile = lax.broadcasted_iota(jnp.int32, (tiles, 128), 0)
     hits = []
@@ -382,7 +385,8 @@
 INNER_ROWS = ((2, 3), (4, 5))
 
 
-def edge_kernel(odd_ref, received_ref, first_ref, edge_ref, sent_one_ref, sent_two_ref):
+def edge_kernel(odd_ref, received_ref, first_ref, *refs):
+    edge_ref, sent_one_ref, sent_two_ref = refs[-3:]
     count = edge_ref.shape[1]
     levels = 72
     tracers = count // levels
@@ -415,7 +419,8 @@
                 ref[at + part : at + part + 1, :] = jnp.sum(total, axis=0, keepdims=True)
 
 
-def inner_kernel(received_ref, first_ref, edge_ref, out_ref, east_ref, west_ref):
+def inner_kernel(received_ref, first_ref, edge_ref, *refs):
+    out_ref, east_ref, west_ref = refs[-3:]
     count = edge_ref.shape[1]
     levels = 72
     tracers = count // levels
@@ -475,7 +480,7 @@
     column_v_ref,
     column_k_ref,
     column_inverse_ref,
-    out_ref,
+    result_ref,
     middle_ref,
     near_ref,
     far_ref,
@@ -484,6 +489,8 @@
     packed_ref,
     column_ref,
     sides_ref,
+    out_ref,
+    copied_ref,
 ):
     levels = k_ref.shape[0] // 8
     tracers = field_ref.shape[0] // (8 * levels)
@@ -626,7 +633,28 @@
         return below, tuple(state)
 
     lax.fori_loop(0, levels // GROUP, final, (zero, (zero,) * tracers))
-    back(levels, tracers, k_ref, inverse_ref, out_ref, ())
+
+    state = [zero] * tracers
+    size = levels // (copied_ref.shape[0] // tracers)
+    copies = []
+    for level in range(levels - 1, -1, -1):
+        spot = pl.ds(level * 8, 8)
+        upper = k_ref[spot, :] * inverse_ref[spot, :]
+        for t in range(tracers):
+            here = pl.ds((t * levels + level) * 8, 8)
+            state[t] = out_ref[here, :] + upper * state[t]
+            out_ref[here, :] = state[t]
+        if level % size == 0:
+            for t in range(tracers):
+                part = pl.ds((t * levels + level) * 8, size * 8)
+                copies.append(
+                    pltpu.make_async_copy(
+                        out_ref.at[part, :], result_ref.at[part, :], copied_ref.at[len(copies)]
+                    )
+                )
+                copies[-1].start()
+    for copy in copies:
+        copy.wait()
 
 
 def swap(one, two, axis, periodic):
@@ -663,11 +691,18 @@
     packed = pl.pallas_call(
         pack_kernel,
         out_shape=jax.ShapeDtypeStruct((tiles, 80, 128), BF16),
-        in_specs=[pl.BlockSpec(memory_space=pltpu.SMEM)]
-        + [pl.BlockSpec(memory_space=pltpu.VMEM)] * 3,
+        in_specs=[pl.BlockSpec(memory_space=pltpu.VMEM)] * 4,
         compiler_params=pltpu.CompilerParams(vmem_limit_bytes=56 << 20),
         name="pack",
-    )(retrieval_counts, kernel_rows, retrieval_misfit, retrieval_columns.reshape(slots // 128, 128))
+    )(
+        retrieval_counts.reshape(1, 1),
+        kernel_rows,
+        retrieval_misfit,
+        retrieval_columns.reshape(slots // 128, 128),
+    )
+    packed, adjoint_in, wind_u, wind_v, diffusion = lax.optimization_barrier(
+        (packed, adjoint_in, wind_u, wind_v, diffusion)
+    )
     received = lax.all_to_all(packed, "lon", split_axis=0, concat_axis=0, tiled=True)
 
     field = adjoint_in.reshape(full.shape)
@@ -708,10 +743,10 @@
         smem=1,
         limit=30,
         name="edge",
-    )(odd, received, first)
+    )(odd, received, first, u, v, inverse, *edges[:2])
     injected, east, west = vmem_call(
         inner_kernel, out_shape=(full, columns_two, columns_two), limit=30, name="inner"
-    )(received, first, edge)
+    )(received, first, edge, u, v, inverse, *edges[:2])
     rows = swap(*sent, "lat", False)
     sent = vmem_call(relay_kernel, out_shape=(columns_sent,) * 2, smem=1, name="relay")(
         odd, *rows, east, west
@@ -723,7 +758,8 @@
         smem=1,
         scratch=(full,)
         + (planes,) * 4
-        + (columns_two, planes, jax.ShapeDtypeStruct((2,) + columns_sent.shape, F32)),
+        + (columns_two, planes, jax.ShapeDtypeStruct((2,) + columns_sent.shape, F32), full),
+        copies=3 * tracers,
         name="last",
     )(odd, injected, u, v, k, inverse, *rows, *columns, west, east, *ring)
     return last.reshape(adjoint_in.shape)

time: 76.7 us -> 75.5 us (0.984)
  local copies, waits for them, and re-layouts: 3.19 us -> 1.24 us
    unnamed x33 -> x22, local copies, waits for them, and re-layouts: 3.19 us -> 1.24 us
where the time goes in v3:
time: 75.5 us; the launch traced here: 75.1 us
  starting transfers between devices  40.2 us (53%)
  Pallas kernels  24.9 us (33%)
  waiting for transfers between devices  7.48 us (10%)
  local copies, waits for them, and re-layouts  1.24 us (2%)
  between operations  1.2 us (2%)
    ppermute x8, starting transfers between devices, swap(): return (lax.ppermute(one, axis, both[0]), lax.ppermute(two, axis, both[1]))  27 us
    pallas_call x8, Pallas kernels, run(): pl.pallas_call(kernel, out_shape=out_shape if copies else outs if is_tupl...  19.6 us
    all_to_all x1, starting transfers between devices, body(): lax.all_to_all(packed, 'lon', split_axis=0, concat_axis=0, tiled=True)  13.2 us
    ppermute x8, waiting for transfers between devices, swap(): return (lax.ppermute(one, axis, both[0]), lax.ppermute(two, axis, both[1]))  7.47 us
    pallas_call x1, Pallas kernels, body(): pl.pallas_call(pack_kernel, out_shape=jax.ShapeDtypeStruct((tiles, 80, 12...  5.33 us
  transfers between devices with their start and end apart: 9, of which 3 were waited for; matrix products, arithmetic and copies ran while one was open for 0% of the time, Pallas kernels for 12%

profile of v3, /device:TPU:32, one launch (start us, length us, event | category | flops | bytes accessed | tf_op | source)
XLA Modules:
  0.0 75.1 jit_solution(11932344500542797395)
XLA Ops:
  0.0 0.0 copy-start.2
  0.0 0.0 copy-start.1
  0.0 0.0 copy-start.3
  0.0 0.0 copy-start.9
  0.0 0.0 copy-start.10
  0.8 5.3 %pack.1 = bf16[32,80,128]{2,1,0:T(8,128)(2,1)} custom-call(s32[1,1]{1,0:T(1,128)} %bitcast.9.count_ref, bf16[72,2048]{1,0:T(8,128)(2,1)} %rows_ref.1, bf16[4,2048]{1,0:T(4,128)(2,1)} %misfit_ref.1, s32[16,128]{1,0:T(8,128)} %bitcast.26), custom_call_target="tpu_custom_call" | custom-call | tf_op jit(solution)/shard_map/pack/pallas_call | solution.py:691
  6.2 13.2 %all-to-all-start = ((bf16[32,80,128]{2,1,0:T(8,128)(2,1)}), bf16[32,80,128]{2,1,0:T(8,128)(2,1)S(1)}, u32[]{:S(2)}, u32[]{:S(2)}) async-start(bf16[32,80,128]{2,1,0:T(8,128)(2,1)} %pack.1), calls=%async_computation | async-start | bytes 1310720 | tf_op jit(solution)/shard_map/all_to_all | solution.py:706
  19.3 0.1 pad_add_fusion.odd_ref
  19.4 0.0 copy-done.2
  19.4 0.0 copy-done.1
  19.4 0.0 copy-done
  19.4 0.0 copy-done.3
  19.4 0.0 copy-done.9
  19.4 0.0 copy-done.10
  19.5 0.0 copy-start.4
  19.5 1.9 %prep.1 = (f32[4,8,128]{2,1,0:T(8,128)S(1)}, f32[504,128]{1,0:T(8,128)S(1)}, f32[504,128]{1,0:T(8,128)S(1)}, f32[7,8,128]{2,1,0:T(8,128)S(1)}, f32[7,8,128]{2,1,0:T(8,128)S(1)}) custom-call(s32[2]{0:T(128)S(1)} %pad_add_fusion.odd_ref, s32[16]{0:T(128)S(1)} %copy-done.10, f32[4,16]{1,0:T(4,128)S(1)} %copy-done.9, f32[2304,128]{1,0:T(8,128)S(1)} %bitcast.24, ...), custom_call_target="tpu_custom_call" | custom-call | tf_op jit(solution)/shard_map/prep/pallas_call | solution.py:25
  21.3 1.9 %collective-permute-start = (f32[504,128]{1,0:T(8,128)S(1)}, f32[504,128]{1,0:T(8,128)S(1)}, u32[]{:S(2)}, u32[]{:S(2)}) collective-permute-start(f32[504,128]{1,0:T(8,128)S(1)} %get-tuple-element.37), channel_id=1, source_target_pairs={{0,32},{32,0},{64,96},{96,64},{128,160},{160,128},{192,224},{224,1... | collective-permute-start | bytes 774152 | tf_op jit(solution)/shard_map/ppermute | solution.py:664
  23.3 2.5 %collective-permute-start.1 = (f32[504,128]{1,0:T(8,128)S(1)}, f32[504,128]{1,0:T(8,128)S(1)}, u32[]{:S(2)}, u32[]{:S(2)}) collective-permute-start(f32[504,128]{1,0:T(8,128)S(1)} %get-tuple-element.38), channel_id=1, source_target_pairs={{32,64},{64,32},{96,128},{128,96},{160,192},{192,160},{224,256},{2... | collective-permute-start | bytes 774152 | tf_op jit(solution)/shard_map/ppermute | solution.py:664
  25.7 3.7 %collective-permute-start.2 = (f32[7,8,128]{2,1,0:T(8,128)S(1)}, f32[7,8,128]{2,1,0:T(8,128)S(1)}, u32[]{:S(2)}, u32[]{:S(2)}) collective-permute-start(f32[7,8,128]{2,1,0:T(8,128)S(1)} %get-tuple-element.39), channel_id=1, source_target_pairs={{0,1},{1,0},{2,3},{3,2},{4,5},{5,4},{6,7},{7,6},{8,9},{9,8},{10,11... | collective-permute-start | bytes 86024 | tf_op jit(solution)/shard_map/ppermute | solution.py:664
  29.4 6.2 %collective-permute-start.3 = (f32[7,8,128]{2,1,0:T(8,128)S(1)}, f32[7,8,128]{2,1,0:T(8,128)S(1)}, u32[]{:S(2)}, u32[]{:S(2)}) collective-permute-start(f32[7,8,128]{2,1,0:T(8,128)S(1)} %get-tuple-element.40), channel_id=1, source_target_pairs={{1,2},{2,1},{3,4},{4,3},{5,6},{6,5},{7,8},{8,7},{9,10},{10,9},{11,... | collective-permute-start | bytes 86024 | tf_op jit(solution)/shard_map/ppermute | solution.py:664
  35.6 0.5 factor.1.inverse_ref.refs_2_
  36.2 0.0 collective-permute-done.2.columns_one_ref
  36.2 2.7 %collective-permute-done.3.columns_two_ref = f32[7,8,128]{2,1,0:T(8,128)S(1)} collective-permute-done((f32[7,8,128]{2,1,0:T(8,128)S(1)}, f32[7,8,128]{2,1,0:T(8,128)S(1)}, u32[]{:S(2)}, u32[]{:S(2)}) %collective-permute-start.3) | collective-permute-done | bytes 28704 | tf_op jit(solution)/shard_map/ppermute | solution.py:664
  38.8 0.0 collective-permute-done.rows_one_ref.refs_3_
  38.8 0.0 collective-permute-done.1.rows_two_ref.refs_4_
  38.8 0.0 copy-done.4
  38.9 2.1 %first.1.first_ref = f32[2304,128]{1,0:T(8,128)S(1)} custom-call(s32[2]{0:T(128)S(1)} %pad_add_fusion.odd_ref, f32[2304,128]{1,0:T(8,128)S(1)} %bitcast.25, f32[4,8,128]{2,1,0:T(8,128)S(1)} %get-tuple-element.36.surface_ref, f32[576,128]{1,0:T(8,128)S(1)} %bitcast.11, f32[576,128]{1,0:T(8,128)S(1)} %bitcast.16, f32[576,128]{1,0:T(8,128)S(1)} %bitcast.22, ...), custom_call_target="tpu_custom_call" | custom-call | tf_op jit(solution)/shard_map/first/pallas_call | solution.py:25
  41.0 0.0 copy-start.5
  41.0 0.6 copy-done.5
  41.6 0.6 copy-done.7
  42.2 0.0 all-to-all-done.received_ref
  42.2 3.4 %edge.1 = (f32[4,288,128]{2,1,0:T(8,128)S(1)}, f32[592,128]{1,0:T(8,128)S(1)}, f32[592,128]{1,0:T(8,128)S(1)}) custom-call(s32[2]{0:T(128)S(1)} %pad_add_fusion.odd_ref, bf16[32,80,128]{2,1,0:T(8,128)(2,1)S(1)} %all-to-all-done.received_ref, f32[2304,128]{1,0:T(8,128)S(1)} %first.1.first_ref, f32[576,128]{1,0:T(8,128)S(1)} %bitcast.12, ...), custom_call_target="tpu_custom_call" | custom-call | tf_op jit(solution)/shard_map/edge/pallas_call | solution.py:25
  45.6 1.9 %collective-permute-start.4 = (f32[592,128]{1,0:T(8,128)S(1)}, f32[592,128]{1,0:T(8,128)S(1)}, u32[]{:S(2)}, u32[]{:S(2)}) collective-permute-start(f32[592,128]{1,0:T(8,128)S(1)} %get-tuple-element.43), channel_id=1, source_target_pairs={{0,32},{32,0},{64,96},{96,64},{128,160},{160,128},{192,224},{224,1... | collective-permute-start | bytes 909320 | tf_op jit(solution)/shard_map/ppermute | solution.py:664
  47.5 3.1 %collective-permute-start.5 = (f32[592,128]{1,0:T(8,128)S(1)}, f32[592,128]{1,0:T(8,128)S(1)}, u32[]{:S(2)}, u32[]{:S(2)}) collective-permute-start(f32[592,128]{1,0:T(8,128)S(1)} %get-tuple-element.44), channel_id=1, source_target_pairs={{32,64},{64,32},{96,128},{128,96},{160,192},{192,160},{224,256},{2... | collective-permute-start | bytes 909320 | tf_op jit(solution)/shard_map/ppermute | solution.py:664
  50.6 0.0 copy-start.6
  50.6 0.0 copy-start.8
  50.6 3.4 %inner.1 = (f32[2304,128]{1,0:T(8,128)S(1)}, f32[40,128]{1,0:T(8,128)S(1)}, f32[40,128]{1,0:T(8,128)S(1)}) custom-call(bf16[32,80,128]{2,1,0:T(8,128)(2,1)S(1)} %all-to-all-done.received_ref, f32[2304,128]{1,0:T(8,128)S(1)} %first.1.first_ref, f32[4,288,128]{2,1,0:T(8,128)S(1)} %get-tuple-element.41.edge_ref, f32[576,128]{1,0:T(8,128)S(1)} %bitcast.13, ...), custom_call_target="tpu_custom_call" | custom-call | tf_op jit(solution)/shard_map/inner/pallas_call | solution.py:25
  54.0 0.0 collective-permute-done.4.one_ref.rows_one_ref
  54.0 2.8 %collective-permute-done.5.two_ref.rows_two_ref = f32[592,128]{1,0:T(8,128)S(1)} collective-permute-done((f32[592,128]{1,0:T(8,128)S(1)}, f32[592,128]{1,0:T(8,128)S(1)}, u32[]{:S(2)}, u32[]{:S(2)}) %collective-permute-start.5) | collective-permute-done | bytes 303136 | tf_op jit(solution)/shard_map/ppermute | solution.py:664
  56.8 0.6 relay.1
  57.4 1.9 %collective-permute-start.6 = (f32[56,128]{1,0:T(8,128)S(1)}, f32[56,128]{1,0:T(8,128)S(1)}, u32[]{:S(2)}, u32[]{:S(2)}) collective-permute-start(f32[56,128]{1,0:T(8,128)S(1)} %get-tuple-element.47), channel_id=1, source_target_pairs={{0,1},{1,0},{2,3},{3,2},{4,5},{5,4},{6,7},{7,6},{8,9},{9,8},{10,11... | collective-permute-start | bytes 86024 | tf_op jit(solution)/shard_map/ppermute | solution.py:664
  59.3 5.9 %collective-permute-start.7 = (f32[56,128]{1,0:T(8,128)S(1)}, f32[56,128]{1,0:T(8,128)S(1)}, u32[]{:S(2)}, u32[]{:S(2)}) collective-permute-start(f32[56,128]{1,0:T(8,128)S(1)} %get-tuple-element.48), channel_id=1, source_target_pairs={{1,2},{2,1},{3,4},{4,3},{5,6},{6,5},{7,8},{8,7},{9,10},{10,9},{11,... | collective-permute-start | bytes 86024 | tf_op jit(solution)/shard_map/ppermute | solution.py:664
  65.2 0.0 copy-done.6
  65.2 0.0 copy-done.8
  65.2 1.2 %ring.1 = (f32[576,128]{1,0:T(8,128)S(1)}, f32[576,128]{1,0:T(8,128)S(1)}, f32[576,128]{1,0:T(8,128)S(1)}, f32[576,128]{1,0:T(8,128)S(1)}, f32[40,128]{1,0:T(8,1...) custom-call(s32[2]{0:T(128)S(1)} %pad_add_fusion.odd_ref, ...), custom_call_target="tpu_custom_call" | custom-call | tf_op jit(solution)/shard_map/ring/pallas_call | solution.py:25
  66.4 0.0 collective-permute-done.6.columns_one_ref
  66.5 2.0 %collective-permute-done.7.columns_two_ref = f32[56,128]{1,0:T(8,128)S(1)} collective-permute-done((f32[56,128]{1,0:T(8,128)S(1)}, f32[56,128]{1,0:T(8,128)S(1)}, u32[]{:S(2)}, u32[]{:S(2)}) %collective-permute-start.7) | collective-permute-done | bytes 28704 | tf_op jit(solution)/shard_map/ppermute | solution.py:664
  68.4 6.5 %last.1 = f32[2304,128]{1,0:T(8,128)} custom-call(s32[2]{0:T(128)S(1)} %pad_add_fusion.odd_ref, f32[2304,128]{1,0:T(8,128)S(1)} %get-tuple-element.42.field_ref, f32[576,128]{1,0:T(8,128)S(1)} %bitcast.14, f32[576,128]{1,0:T(8,128)S(1)} %bitcast.19, f32[576,128]{1,0:T(8,128)S(1)} %bitcast.23, f32[576,128]{1,0:T(8,128)S(1)} %factor.1.inverse_ref.refs_2_, ...), custom_call_target="tpu_custom_call" | custom-call | tf_op jit(solution)/shard_map/last/pallas_call | solution.py:25
  (2 shorter events, 0.0 us)
Async XLA Ops:
  0.0 19.4 %copy-start.2 = (f32[72,8,128]{2,1,0:T(8,128)S(1)}, f32[72,8,128]{2,1,0:T(8,128)}, u32[]{:S(2)}) copy-start(f32[72,8,128]{2,1,0:T(8,128)} %param.13) | copy-start | bytes 884740
  0.0 19.4 %copy-start.1 = (f32[72,8,128]{2,1,0:T(8,128)S(1)}, f32[72,8,128]{2,1,0:T(8,128)}, u32[]{:S(2)}) copy-start(f32[72,8,128]{2,1,0:T(8,128)} %param.12) | copy-start | bytes 884740
  0.0 19.4 %copy-start = (f32[72,8,128]{2,1,0:T(8,128)S(1)}, f32[72,8,128]{2,1,0:T(8,128)}, u32[]{:S(2)}) copy-start(f32[72,8,128]{2,1,0:T(8,128)} %param.11) | copy-start | bytes 884740
  0.0 19.4 %copy-start.3 = (f32[4,72,8,128]{3,2,1,0:T(8,128)S(1)}, f32[4,72,8,128]{3,2,1,0:T(8,128)}, u32[]{:S(2)}) copy-start(f32[4,72,8,128]{3,2,1,0:T(8,128)} %param.10) | copy-start | bytes 3538948
  0.0 19.4 %copy-start.9 = (f32[4,16]{1,0:T(4,128)S(1)}, f32[4,16]{1,0:T(4,128)}, u32[]{:S(2)}) copy-start(f32[4,16]{1,0:T(4,128)} %weights_ref.1) | copy-start | bytes 772
  0.0 19.4 %copy-start.10 = (s32[16]{0:T(128)S(1)}, s32[16]{0:T(128)}, u32[]{:S(2)}) copy-start(s32[16]{0:T(128)} %cells_ref.1) | copy-start | bytes 196
  6.2 36.0 %all-to-all-start = ((bf16[32,80,128]{2,1,0:T(8,128)(2,1)}), bf16[32,80,128]{2,1,0:T(8,128)(2,1)S(1)}, u32[]{:S(2)}, u32[]{:S(2)}) async-start(bf16[32,80,128]{2,1,0:T(8,128)(2,1)} %pack.1), calls=%async_computation | async-start | bytes 1310720 | tf_op jit(solution)/shard_map/all_to_all | solution.py:706
  19.5 19.4 %copy-start.4 = (f32[4,72,8,128]{3,2,1,0:T(8,128)S(1)}, f32[4,72,8,128]{3,2,1,0:T(8,128)}, u32[]{:S(2)}) copy-start(f32[4,72,8,128]{3,2,1,0:T(8,128)} %param.10) | copy-start | bytes 3538948
  21.3 17.5 %collective-permute-start = (f32[504,128]{1,0:T(8,128)S(1)}, f32[504,128]{1,0:T(8,128)S(1)}, u32[]{:S(2)}, u32[]{:S(2)}) collective-permute-start(f32[504,128]{1,0:T(8,128)S(1)} %get-tuple-element.37), channel_id=1, source_target_pairs={{0,32},{32,0},{64,96},{96,64},{128,160},{160,128},{192,224},{224,1... | collective-permute-start | bytes 774152 | tf_op jit(solution)/shard_map/ppermute | solution.py:664
  23.3 15.6 %collective-permute-start.1 = (f32[504,128]{1,0:T(8,128)S(1)}, f32[504,128]{1,0:T(8,128)S(1)}, u32[]{:S(2)}, u32[]{:S(2)}) collective-permute-start(f32[504,128]{1,0:T(8,128)S(1)} %get-tuple-element.38), channel_id=1, source_target_pairs={{32,64},{64,32},{96,128},{128,96},{160,192},{192,160},{224,256},{2... | collective-permute-start | bytes 774152 | tf_op jit(solution)/shard_map/ppermute | solution.py:664
  25.7 10.4 %collective-permute-start.2 = (f32[7,8,128]{2,1,0:T(8,128)S(1)}, f32[7,8,128]{2,1,0:T(8,128)S(1)}, u32[]{:S(2)}, u32[]{:S(2)}) collective-permute-start(f32[7,8,128]{2,1,0:T(8,128)S(1)} %get-tuple-element.39), channel_id=1, source_target_pairs={{0,1},{1,0},{2,3},{3,2},{4,5},{5,4},{6,7},{7,6},{8,9},{9,8},{10,11... | collective-permute-start | bytes 86024 | tf_op jit(solution)/shard_map/ppermute | solution.py:664
  29.4 9.4 %collective-permute-start.3 = (f32[7,8,128]{2,1,0:T(8,128)S(1)}, f32[7,8,128]{2,1,0:T(8,128)S(1)}, u32[]{:S(2)}, u32[]{:S(2)}) collective-permute-start(f32[7,8,128]{2,1,0:T(8,128)S(1)} %get-tuple-element.40), channel_id=1, source_target_pairs={{1,2},{2,1},{3,4},{4,3},{5,6},{6,5},{7,8},{8,7},{9,10},{10,9},{11,... | collective-permute-start | bytes 86024 | tf_op jit(solution)/shard_map/ppermute | solution.py:664
  41.0 0.6 copy-start.5
  41.6 0.6 copy-start.7
  45.6 8.4 %collective-permute-start.4 = (f32[592,128]{1,0:T(8,128)S(1)}, f32[592,128]{1,0:T(8,128)S(1)}, u32[]{:S(2)}, u32[]{:S(2)}) collective-permute-start(f32[592,128]{1,0:T(8,128)S(1)} %get-tuple-element.43), channel_id=1, source_target_pairs={{0,32},{32,0},{64,96},{96,64},{128,160},{160,128},{192,224},{224,1... | collective-permute-start | bytes 909320 | tf_op jit(solution)/shard_map/ppermute | solution.py:664
  47.5 9.3 %collective-permute-start.5 = (f32[592,128]{1,0:T(8,128)S(1)}, f32[592,128]{1,0:T(8,128)S(1)}, u32[]{:S(2)}, u32[]{:S(2)}) collective-permute-start(f32[592,128]{1,0:T(8,128)S(1)} %get-tuple-element.44), channel_id=1, source_target_pairs={{32,64},{64,32},{96,128},{128,96},{160,192},{192,160},{224,256},{2... | collective-permute-start | bytes 909320 | tf_op jit(solution)/shard_map/ppermute | solution.py:664
  50.6 14.6 %copy-start.6 = (f32[7,8,128]{2,1,0:T(8,128)S(1)}, f32[7,8,128]{2,1,0:T(8,128)}, u32[]{:S(2)}) copy-start(f32[7,8,128]{2,1,0:T(8,128)} %copy-done.5) | copy-start | bytes 86020
  50.6 14.6 %copy-start.8 = (f32[7,8,128]{2,1,0:T(8,128)S(1)}, f32[7,8,128]{2,1,0:T(8,128)}, u32[]{:S(2)}) copy-start(f32[7,8,128]{2,1,0:T(8,128)} %copy-done.7) | copy-start | bytes 86020
  57.4 9.1 %collective-permute-start.6 = (f32[56,128]{1,0:T(8,128)S(1)}, f32[56,128]{1,0:T(8,128)S(1)}, u32[]{:S(2)}, u32[]{:S(2)}) collective-permute-start(f32[56,128]{1,0:T(8,128)S(1)} %get-tuple-element.47), channel_id=1, source_target_pairs={{0,1},{1,0},{2,3},{3,2},{4,5},{5,4},{6,7},{7,6},{8,9},{9,8},{10,11... | collective-permute-start | bytes 86024 | tf_op jit(solution)/shard_map/ppermute | solution.py:664
  59.3 9.1 %collective-permute-start.7 = (f32[56,128]{1,0:T(8,128)S(1)}, f32[56,128]{1,0:T(8,128)S(1)}, u32[]{:S(2)}, u32[]{:S(2)}) collective-permute-start(f32[56,128]{1,0:T(8,128)S(1)} %get-tuple-element.48), channel_id=1, source_target_pairs={{1,2},{2,1},{3,4},{4,3},{5,6},{6,5},{7,8},{8,7},{9,10},{10,9},{11,... | collective-permute-start | bytes 86024 | tf_op jit(solution)/shard_map/ppermute | solution.py:664
